TPU v7x, 256 devices: a whole 4x4x8 slice. The times are simulated.
256 devices in a mesh: dp: 16 (over y, z_lo), mp: 4 (over x), expert: 4 (over z_hi, core).
Axes of the slice: x: 4, y: 4, z: 8 (z_hi: 2, z_lo: 4; z = z_hi * 4 + z_lo), core: 2. Of those that a mesh axis runs over, the one named last changes fastest.
Arguments:
- tokens: bfloat16 [24576, 1536], P(('dp', 'expert')), may hold values from -24 to 24
- segments: int32 [24576], replicated, may hold values from 0 to 47, never falling along the last dimension, each value on 1 to 1024 neighbouring positions
- norm_gains: float32 [2, 1536], replicated, may hold values from 0.1 to 1.9
- query_weight: bfloat16 [1536, 1536], P(None, 'mp'), may hold values from -8 to 8
- key_value_matrix: bfloat16 [2, 1536, 256], replicated, may hold values from -1 to 1
- output_weight: bfloat16 [1536, 1536], P('mp'), may hold values from -1 to 1
- trainer_gateup: float32 [16, 1536, 1536], P(('mp', 'expert'), 'dp'), may hold values from -0.15625 to 0.15625
- trainer_down: float32 [16, 768, 1536], P(('mp', 'expert'), 'dp'), may hold values from -0.21875 to 0.21875
- routes: int32 [24576, 4], P(('dp', 'expert')), may hold values from 0 to 15, all different within a row; in each aligned block of 96 rows (0 to 95, 96 to 191, ...) at most 48 rows name the same one
- route_weights: float32 [24576, 4], P(('dp', 'expert')), may hold values from 0.05 to 0.6
Outputs:
- layer_out: bfloat16 [64, 4, 96, 1536], P(('dp', 'expert'), 'mp')
Inputs may be any that keep to these rules, and one draw needn't show every extreme that they name: `segments`: prompt numbers never fall along the positions; each prompt covers 1 to 1024 positions, and one covers exactly 1024. `routes`: the 4 experts of a token differ; in each aligned block of 96 rows no expert is named more than 48 times, a bound that some block reaches.
All inputs are finite; a program needn't handle non-finite values.
Results may differ from a plain program's by a relative error of at most 0.014.
Values may be sent and summed in bfloat16 or wider, within the bound.
A program may use at most 64 MiB of HBM per device.

v0:
```python
import math

import jax
import jax.numpy as jnp
from jax import lax
from jax.sharding import PartitionSpec as P

MODEL_WIDTH = 1536
QUERY_HEADS = 12
KEY_VALUE_HEADS = 2
HEAD_SIZE = 128
FF = 768
TOPK = 4
PROMPT_MAX = 1024


def shifted(value, axis, steps):
    count = lax.axis_size(axis)
    initial, last = (max(0, -steps), min(count, count - steps))
    return lax.ppermute(value, axis, [(source, source + steps) for source in range(initial, last)])


def rms_scale(values, scaling):
    widened = values.astype(jnp.float32)
    return (
        widened * lax.rsqrt(jnp.mean(widened * widened, axis=-1, keepdims=True) + 1e-06) * scaling
    )


def slot_index(chosen, experts_count, capacity):
    flattened = chosen.reshape(-1)
    onehot = (flattened[:, None] == jnp.arange(experts_count, dtype=jnp.int32)[None, :]).astype(
        jnp.int32
    )
    before = jnp.cumsum(onehot, axis=0) - onehot
    return flattened * capacity + jnp.sum(before * onehot, axis=1)


def body(
    tokens,
    segments,
    norm_gains,
    query_weight,
    key_value_matrix,
    output_weight,
    trainer_gateup,
    trainer_down,
    routes,
    route_weights,
):
    gateup_full, down_full = (
        lax.all_gather(trainer_gateup.astype(jnp.bfloat16), "dp", axis=1, tiled=True),
        lax.all_gather(trainer_down.astype(jnp.bfloat16), "dp", axis=1, tiled=True),
    )
    own_rows = tokens.shape[0]
    head_group_index = lax.axis_index(("dp", "expert"))
    column_position = lax.axis_index("mp")
    first_row = head_group_index * own_rows
    local_heads = query_weight.shape[1] // HEAD_SIZE
    normalized_input = rms_scale(tokens, norm_gains[0]).astype(jnp.bfloat16)
    query_rows = jnp.dot(normalized_input, query_weight, preferred_element_type=jnp.float32).astype(
        jnp.bfloat16
    )
    paired_head_index = column_position * local_heads // (QUERY_HEADS // KEY_VALUE_HEADS)
    pair_weight = lax.dynamic_index_in_dim(key_value_matrix, paired_head_index, 0, keepdims=False)
    key_values = jnp.dot(normalized_input, pair_weight, preferred_element_type=jnp.float32).astype(
        jnp.bfloat16
    )
    query_pos = first_row + jnp.arange(own_rows, dtype=jnp.int32)
    query_segment = lax.dynamic_slice_in_dim(segments, first_row, own_rows, 0)
    shaped_queries = query_rows.reshape(own_rows, local_heads, HEAD_SIZE)
    start_state = (
        jnp.full((local_heads, own_rows), -1e30, jnp.float32),
        jnp.zeros((local_heads, own_rows), jnp.float32),
        jnp.zeros((local_heads, own_rows, HEAD_SIZE), jnp.float32),
    )
    pieces_back = (PROMPT_MAX - 1) // own_rows + 1
    earlier = [key_values]
    for offset in range(1, pieces_back + 1):
        earlier.insert(0, shifted(key_values, ("dp", "expert"), offset))
    key_pos = (
        first_row
        - pieces_back * own_rows
        + jnp.arange((pieces_back + 1) * own_rows, dtype=jnp.int32)
    )
    key_segment = jnp.where(key_pos >= 0, segments[jnp.maximum(key_pos, 0)], -1)
    block_pairs = jnp.concatenate(earlier, axis=0)
    highest, denominator, accumulated = start_state
    scores = jnp.einsum(
        "rhd,nd->hrn",
        shaped_queries,
        block_pairs[:, :HEAD_SIZE],
        preferred_element_type=jnp.float32,
    ) / math.sqrt(HEAD_SIZE)
    allowed = (
        (query_segment[:, None] == key_segment[None, :]) & (key_pos[None, :] <= query_pos[:, None])
    )[None]
    newest = jnp.maximum(highest, jnp.max(jnp.where(allowed, scores, -1e30), axis=-1))
    weights = jnp.where(allowed, jnp.exp(scores - newest[..., None]), 0.0)
    denominator = jnp.sum(weights, axis=-1)
    accumulated = jnp.einsum(
        "hrn,nd->hrd",
        weights.astype(jnp.bfloat16),
        block_pairs[:, HEAD_SIZE:],
        preferred_element_type=jnp.float32,
    )
    carried = (newest, denominator, accumulated)
    highest, denominator, accumulated = carried
    attended = (
        jnp.transpose(accumulated / denominator[..., None], (1, 0, 2))
        .reshape(own_rows, local_heads * HEAD_SIZE)
        .astype(jnp.bfloat16)
    )
    part_rows = own_rows // lax.axis_size("mp")
    attention_out = lax.psum_scatter(
        jnp.dot(attended, output_weight, preferred_element_type=jnp.float32).astype(jnp.bfloat16),
        "mp",
        scatter_dimension=0,
        tiled=True,
    ).astype(jnp.float32)
    part_start = column_position * part_rows
    middle = (
        lax.dynamic_slice_in_dim(tokens, part_start, part_rows, 0).astype(jnp.float32)
        + attention_out
    ).astype(jnp.bfloat16)
    expert_input = rms_scale(middle, norm_gains[1]).astype(jnp.bfloat16)
    chosen = lax.dynamic_slice_in_dim(routes, part_start, part_rows, 0)
    gate_values = lax.dynamic_slice_in_dim(route_weights, part_start, part_rows, 0)
    experts_count = lax.axis_size(("mp", "expert"))
    capacity = 2 * part_rows * TOPK // experts_count
    slot_rows = slot_index(chosen, experts_count, capacity)
    buffer = (
        jnp.zeros((experts_count * capacity, MODEL_WIDTH), jnp.bfloat16)
        .at[slot_rows]
        .set(jnp.repeat(expert_input, TOPK, axis=0))
        .reshape(experts_count, capacity, MODEL_WIDTH)
    )
    received = lax.all_to_all(buffer, ("mp", "expert"), split_axis=0, concat_axis=0, tiled=True)
    senders = received.shape[0]
    slots_here = received.shape[1]
    projected = jnp.dot(
        received.reshape(senders * slots_here, MODEL_WIDTH),
        gateup_full[0],
        preferred_element_type=jnp.float32,
    )
    hidden = (jax.nn.relu(projected[:, :FF]) * projected[:, FF:]).astype(jnp.bfloat16)
    produced = (
        jnp.dot(hidden, down_full[0], preferred_element_type=jnp.float32)
        .astype(jnp.bfloat16)
        .reshape(senders, slots_here, MODEL_WIDTH)
    )
    returned = lax.all_to_all(produced, ("mp", "expert"), split_axis=0, concat_axis=0, tiled=True)
    picked = (
        returned.reshape(experts_count * capacity, MODEL_WIDTH)[slot_rows]
        .reshape(part_rows, TOPK, MODEL_WIDTH)
        .astype(jnp.float32)
    )
    layer = (middle.astype(jnp.float32) + jnp.sum(gate_values[..., None] * picked, axis=1)).astype(
        jnp.bfloat16
    )
    return layer.reshape(1, 1, part_rows, MODEL_WIDTH)


def solution(mesh):
    in_specs = (
        P(("dp", "expert"), None),
        P(),
        P(),
        P(None, "mp"),
        P(),
        P("mp", None),
        P(("mp", "expert"), "dp", None),
        P(("mp", "expert"), "dp", None),
        P(("dp", "expert"), None),
        P(("dp", "expert"), None),
    )
    out_specs = P(("dp", "expert"), "mp", None, None)
    return jax.shard_map(body, mesh=mesh, in_specs=in_specs, out_specs=out_specs, check_vma=False)
```

profile of v0, /device:TPU:32, one launch (start us, length us, event | category | flops | bytes accessed | tf_op | source)
XLA Modules:
  0.0 394.1 jit_solution(15750266479118652651)
XLA Ops:
  7.4 0.0 copy-start
  7.4 0.0 copy-start.1
  7.4 0.0 reduce-scatter.2.cloned.1.call-start
  7.4 0.9 slice_reduce_fusion.1
  8.3 1.6 fusion.10
  9.9 0.0 copy-done
  9.9 1.8 convolution_convert_fusion.3
  11.7 7.6 %collective-permute-start = (bf16[384,256]{1,0:T(8,128)(2,1)S(1)}, bf16[384,256]{1,0:T(8,128)(2,1)S(1)}, u32[]{:S(2)}, u32[]{:S(2)}) collective-permute-start(bf16[384,256]{1,0:T(8,128)(2,1)S(1)} %convolution_convert_fusion.3), channel_id=1, source_target_pairs={{0,3},{1,16},{2,17},{3,18},{16,19},{17,32},{18,33},{19,34},{32,35}... | collective-permute-start | bytes 589832 | tf_op jit(solution)/shard_map/ppermute | solution.py:20
  19.3 2.5 collective-permute-start.1
  21.8 2.8 collective-permute-start.2
  24.6 0.0 copy-done.1
  24.6 0.1 dynamic_slice.17
  24.7 8.4 %gather_fusion = s32[1536]{0:T(1024)S(1)} fusion(s32[24576]{0:T(1024)S(1)} %copy-done.1, s32[2048]{0:T(1024)S(1)} %pad_clamp_fusion), kind=kCustom, calls=%fused_computation | custom fusion | bytes 18432 | tf_op jit(solution)/shard_map/gather | solution.py:86
  33.1 1.1 compare_and_fusion
  34.2 0.0 copy-done.2
  34.2 2.2 convolution_convert_fusion.2
  36.4 0.0 collective-permute-done
  36.4 8.0 %collective-permute-done.1 = bf16[384,256]{1,0:T(8,128)(2,1)S(1)} collective-permute-done((bf16[384,256]{1,0:T(8,128)(2,1)S(1)}, bf16[384,256]{1,0:T(8,128)(2,1)S(1)}, u32[]{:S(2)}, u32[]{:S(2)}) %collective-permute-start.1) | collective-permute-done | bytes 196640 | tf_op jit(solution)/shard_map/ppermute | solution.py:20
  44.4 1.4 collective-permute-done.2
  45.8 1.0 pad_maximum_fusion
  46.8 1.5 fusion
  48.3 1.5 fusion.3
  49.9 1.7 fusion.25
  51.6 0.0 copy-start.4
  51.6 0.0 copy-done.3
  51.6 1.9 convolution_convert_fusion.1
  53.4 0.0 reduce-scatter.2.cloned.1.call-update
  53.5 0.2 all-gather.3.cloned.1.call-start
  53.7 0.0 copy-done.4
  53.7 0.7 convert_element_type.83
  54.5 0.0 all-gather.3.cloned.1.call-update
  54.5 0.8 broadcast_multiply_fusion
  55.3 0.1 copy.20
  55.4 0.1 eq.49
  55.5 0.1 eq.45
  55.6 0.9 reduce-window.6
  56.5 0.2 slice_reduce_fusion
  56.7 0.1 copy.19
  56.8 0.1 mul.97
  56.9 0.1 fusion.40
  57.1 21.6 %reduce-scatter.2.cloned.1.call-done = bf16[96,1536]{1,0:T(8,128)(2,1)} async-done(((bf16[384,1536]{1,0:T(8,128)(2,1)}), bf16[96,1536]{1,0:T(8,128)(2,1)}) %reduce-scatter.2.cloned.1.call-update) | async-done | bytes 294928 | tf_op jit(solution)/shard_map/reduce_scatter | solution.py:115
  78.7 1.2 fusion.30
  79.9 0.1 fusion.32
  80.0 0.3 broadcast_in_dim.51
  80.3 1.2 reshape.200
  81.5 4.9 %scatter_custom_fusion = bf16[768,1536]{1,0:T(8,128)(2,1)} fusion(s32[384]{0:T(512)S(1)} %fusion.42, bf16[384,1536]{1,0:T(8,128)(2,1)} %reshape.200, bf16[]{:T(256)} %constant.74.clone.1), kind=kCustom, calls=%fused_computation.30 | custom fusion | bytes 2359808 | tf_op jit(solution)/shard_map/scatter | solution.py:135
  86.4 7.3 %all-to-all-start = ((bf16[16,48,1536]{2,1,0:T(8,128)(2,1)}), bf16[16,48,1536]{2,1,0:T(8,128)(2,1)}, u32[]{:S(2)}, u32[]{:S(2)}) async-start(bf16[16,48,1536]{2,1,0:T(8,128)(2,1)} %bitcast.77), calls=%async_computation.1 | async-start | bytes 4718592 | tf_op jit(solution)/shard_map/all_to_all | solution.py:138
  93.7 0.0 all-gather.5.cloned.1.call-start
  93.8 0.0 copy-done.5
  93.8 0.7 convert_element_type.85
  94.5 0.0 all-gather.5.cloned.1.call-update
  94.5 109.9 %all-to-all-done = bf16[16,48,1536]{2,1,0:T(8,128)(2,1)} async-done(((bf16[16,48,1536]{2,1,0:T(8,128)(2,1)}), bf16[16,48,1536]{2,1,0:T(8,128)(2,1)}, u32[]{:S(2)}, u32[]{:S(2)}) %all-to-all-start) | async-done | bytes 2359328 | tf_op jit(solution)/shard_map/all_to_all | solution.py:138
  204.4 9.4 %all-gather.3.cloned.1.call-done = bf16[1,1536,1536]{2,1,0:T(8,128)(2,1)} async-done(((bf16[1,96,1536]{2,1,0:T(8,128)(2,1)}), bf16[1,1536,1536]{2,1,0:T(8,128)(2,1)}) %all-gather.3.cloned.1.call-update) | async-done | bytes 4718608 | tf_op jit(solution)/shard_map/all_gather | solution.py:52
  213.8 9.0 %fusion.5 = f32[768,1536]{1,0:T(8,128)} fusion(bf16[768,1536]{1,0:T(8,128)(2,1)} %bitcast.10, bf16[1,1536,1536]{2,1,0:T(8,128)(2,1)} %all-gather.3.cloned.1.call-done), kind=kOutput, calls=%fused_computation.10 | convolution fusion | flops 3623878656 | bytes 11796480 | tf_op jit(solution)/shard_map/dot_general | solution.py:141
  222.8 82.1 %all-gather.5.cloned.1.call-done = bf16[1,768,1536]{2,1,0:T(8,128)(2,1)} async-done(((bf16[1,48,1536]{2,1,0:T(8,128)(2,1)}), bf16[1,768,1536]{2,1,0:T(8,128)(2,1)}) %all-gather.5.cloned.1.call-update) | async-done | bytes 2359312 | tf_op jit(solution)/shard_map/all_gather | solution.py:53
  304.9 6.5 %convolution_convert_fusion = bf16[768,1536]{1,0:T(8,128)(2,1)} fusion(bf16[1,768,1536]{2,1,0:T(8,128)(2,1)} %all-gather.5.cloned.1.call-done, f32[768,1536]{1,0:T(8,128)} %fusion.5), kind=kOutput, calls=%fused_computation.14 | convolution fusion | flops 1814888448 | bytes 9437184 | tf_op jit(solution)/shard_map/dot_general | solution.py:148
  311.4 6.7 %all-to-all-start.1 = ((bf16[16,48,1536]{2,1,0:T(8,128)(2,1)}), bf16[16,48,1536]{2,1,0:T(8,128)(2,1)}, u32[]{:S(2)}, u32[]{:S(2)}) async-start(bf16[16,48,1536]{2,1,0:T(8,128)(2,1)} %bitcast.78), calls=%async_computation.2 | async-start | bytes 4718592 | tf_op jit(solution)/shard_map/all_to_all | solution.py:152
  318.1 0.8 constant_dynamic-slice_fusion.1
  318.9 0.1 copy.18
  319.0 56.1 %all-to-all-done.1 = bf16[16,48,1536]{2,1,0:T(8,128)(2,1)} async-done(((bf16[16,48,1536]{2,1,0:T(8,128)(2,1)}), bf16[16,48,1536]{2,1,0:T(8,128)(2,1)}, u32[]{:S(2)}, u32[]{:S(2)}) %all-to-all-start.1) | async-done | bytes 2359328 | tf_op jit(solution)/shard_map/all_to_all | solution.py:152
  375.0 5.7 %gather_fusion.1 = bf16[384,1536]{1,0:T(8,128)(2,1)S(1)} fusion(bf16[768,1536]{1,0:T(8,128)(2,1)} %bitcast.14, s32[1024]{0:T(1024)S(1)} %pad_clamp_fusion.1), kind=kCustom, calls=%fused_computation.1 | custom fusion | bytes 2360832 | tf_op jit(solution)/shard_map/gather | solution.py:154
  380.7 1.8 reshape.179
  382.5 3.4 multiply_reduce_fusion
  385.9 0.8 fusion.37
  (14 shorter events, 0.1 us)
Async XLA Ops:
  7.4 2.5 copy-start
  7.4 17.3 %copy-start.1 = (s32[24576]{0:T(1024)S(1)}, s32[24576]{0:T(1024)}, u32[]{:S(2)}) copy-start(s32[24576]{0:T(1024)} %param.11) | copy-start | bytes 294916
  7.4 71.3 %reduce-scatter.2.cloned.1.call-start = ((), (), s32[]{:S(2)}) async-start(), calls=%async_computation.3 | async-start | bytes 1474560 | tf_op jit(solution)/shard_map/reduce_scatter | solution.py:115
  11.7 24.8 %collective-permute-start = (bf16[384,256]{1,0:T(8,128)(2,1)S(1)}, bf16[384,256]{1,0:T(8,128)(2,1)S(1)}, u32[]{:S(2)}, u32[]{:S(2)}) collective-permute-start(bf16[384,256]{1,0:T(8,128)(2,1)S(1)} %convolution_convert_fusion.3), channel_id=1, source_target_pairs={{0,3},{1,16},{2,17},{3,18},{16,19},{17,32},{18,33},{19,34},{32,35}... | collective-permute-start | bytes 589832 | tf_op jit(solution)/shard_map/ppermute | solution.py:20
  19.3 25.1 %collective-permute-start.1 = (bf16[384,256]{1,0:T(8,128)(2,1)S(1)}, bf16[384,256]{1,0:T(8,128)(2,1)S(1)}, u32[]{:S(2)}, u32[]{:S(2)}) collective-permute-start(bf16[384,256]{1,0:T(8,128)(2,1)S(1)} %convolution_convert_fusion.3), channel_id=1, source_target_pairs={{0,2},{1,3},{2,16},{3,17},{16,18},{17,19},{18,32},{19,33},{32,34},... | collective-permute-start | bytes 589832 | tf_op jit(solution)/shard_map/ppermute | solution.py:20
  21.8 24.0 %collective-permute-start.2 = (bf16[384,256]{1,0:T(8,128)(2,1)S(1)}, bf16[384,256]{1,0:T(8,128)(2,1)}, u32[]{:S(2)}, u32[]{:S(2)}) collective-permute-start(bf16[384,256]{1,0:T(8,128)(2,1)S(1)} %convolution_convert_fusion.3), channel_id=1, source_target_pairs={{0,1},{1,2},{2,3},{3,16},{16,17},{17,18},{18,19},{19,32},{32,33},{... | collective-permute-start | bytes 589832 | tf_op jit(solution)/shard_map/ppermute | solution.py:20
  24.7 9.5 %copy-start.2 = (bf16[384,1536]{1,0:T(8,128)(2,1)S(1)}, bf16[384,1536]{1,0:T(8,128)(2,1)}, u32[]{:S(2)}) copy-start(bf16[384,1536]{1,0:T(8,128)(2,1)} %param.10) | copy-start | bytes 3538948
  49.9 1.7 copy-start.3
  51.6 2.1 copy-start.4
  53.5 160.3 %all-gather.3.cloned.1.call-start = ((), (), s32[]{:S(2)}) async-start(), calls=%async_computation.4 | async-start | bytes 5013504 | tf_op jit(solution)/shard_map/all_gather | solution.py:52
  86.4 7.4 %copy-start.5 = (f32[1,48,1536]{2,1,0:T(8,128)S(1)}, f32[1,48,1536]{2,1,0:T(8,128)}, u32[]{:S(2)}) copy-start(f32[1,48,1536]{2,1,0:T(8,128)} %param.17) | copy-start | bytes 884740
  86.4 118.0 %all-to-all-start = ((bf16[16,48,1536]{2,1,0:T(8,128)(2,1)}), bf16[16,48,1536]{2,1,0:T(8,128)(2,1)}, u32[]{:S(2)}, u32[]{:S(2)}) async-start(bf16[16,48,1536]{2,1,0:T(8,128)(2,1)} %bitcast.77), calls=%async_computation.1 | async-start | bytes 4718592 | tf_op jit(solution)/shard_map/all_to_all | solution.py:138
  93.7 211.2 %all-gather.5.cloned.1.call-start = ((), (), s32[]{:S(2)}) async-start(), calls=%async_computation.5 | async-start | bytes 2506752 | tf_op jit(solution)/shard_map/all_gather | solution.py:53
  311.4 63.6 %all-to-all-start.1 = ((bf16[16,48,1536]{2,1,0:T(8,128)(2,1)}), bf16[16,48,1536]{2,1,0:T(8,128)(2,1)}, u32[]{:S(2)}, u32[]{:S(2)}) async-start(bf16[16,48,1536]{2,1,0:T(8,128)(2,1)} %bitcast.78), calls=%async_computation.2 | async-start | bytes 4718592 | tf_op jit(solution)/shard_map/all_to_all | solution.py:152
Sparse Core Ops, SparseCore 0:
  53.6 25.0 reduce-scatter.1
Sparse Core Ops, SparseCore 1:
  55.7 158.0 all-gather.2
  215.4 89.4 all-gather.4
where the time goes:
time: 397 us; the launch traced here: 394 us
  waiting for transfers between devices  289 us (73%)
  starting transfers between devices  27.1 us (7%)
  local copies, waits for them, and re-layouts  24.8 us (6%)
  matrix products  24.6 us (6%)
  between operations  15.1 us (4%)
  other arithmetic  14 us (4%)
    all_to_all x1, waiting for transfers between devices, body(): lax.all_to_all(buffer, ('mp', 'expert'), split_axis=0, concat_axis=0, til...  110 us
    all_gather x1, waiting for transfers between devices, body(): lax.all_gather(trainer_down.astype(jnp.bfloat16), 'dp', axis=1, tiled=True)  82.1 us
    all_to_all x1, waiting for transfers between devices, body(): lax.all_to_all(produced, ('mp', 'expert'), split_axis=0, concat_axis=0, t...  56.1 us
    reduce_scatter x1, waiting for transfers between devices, body(): lax.psum_scatter(jnp.dot(attended, output_weight, preferred_element_type=...  21.6 us
    ppermute x3, starting transfers between devices, shifted(): lax.ppermute(value, axis, [(source, source + steps) for source in range(i...  12.9 us
    all_gather x1, waiting for transfers between devices, body(): lax.all_gather(trainer_gateup.astype(jnp.bfloat16), 'dp', axis=1, tiled=T...  9.41 us
    ppermute x3, waiting for transfers between devices, shifted(): lax.ppermute(value, axis, [(source, source + steps) for source in range(i...  9.36 us
    dot_general x1, matrix products, body(): jnp.dot(received.reshape(senders * slots_here, MODEL_WIDTH), gateup_full[...  9.03 us
  transfers between devices with their start and end apart: 8, of which 7 were waited for; matrix products, arithmetic and copies ran while one was open for 8% of the time, Pallas kernels for 0%

commit v1 on v0

--- a/solution.py
+++ b/solution.py
@@ -1,8 +1,12 @@
+import functools
+import heapq
 import math
 
 import jax
 import jax.numpy as jnp
 from jax import lax
+from jax.experimental import pallas as pl
+from jax.experimental.pallas import tpu as pltpu
 from jax.sharding import PartitionSpec as P
 
 MODEL_WIDTH = 1536
@@ -12,6 +16,157 @@
 FF = 768
 TOPK = 4
 PROMPT_MAX = 1024
+
+
+LINKS = ("y+", "y-", "z+", "z-")
+AXES = ("dp", "mp", "expert")
+MESH = pl.DeviceIdType.MESH
+
+
+def column_ring(moves, rank, tag, piece, halves, dy, have):
+    got = {0: have}
+    up, down = have, have
+    for s in range(1, 4):
+        moves.append(("z+", (dy, 1 - s), piece, up, (rank, tag, s)))
+        up = got[-s] = [len(moves) - 1]
+        moves.append(("z-", (dy, s - 1), piece, down, (rank, tag, s)))
+        down = got[s] = [len(moves) - 1]
+    moves.append(("z+", (dy, -3), halves[0], up, (rank, tag, 4)))
+    moves.append(("z-", (dy, 3), halves[1], down, (rank, tag, 4)))
+    got[4] = [len(moves) - 2, len(moves) - 1]
+    return got
+
+
+def row_ring(moves, rank, tag, piece, halves, dz, have, late):
+    start = len(moves)
+    moves.append(("y+", (0, dz), piece, have, (rank, tag, 1 + late)))
+    moves.append(("y-", (0, dz), piece, have, (rank, tag, 1 + late)))
+    moves.append(("y+", (-1, dz), halves[0], [start], (rank, tag, 2 + late)))
+    moves.append(("y-", (1, dz), halves[1], [start + 1], (rank, tag, 2 + late)))
+    return {0: have, -1: [start], 1: [start + 1], 2: [start + 2, start + 3]}
+
+
+def gather_moves(pieces):
+    moves = []
+    for rank, order, piece, halves in pieces:
+        if order == "zy":
+            got = column_ring(moves, rank, 0, piece, halves, 0, [])
+            for late, dz in enumerate((0, -1, 1, -2, 2, -3, 3, 4)):
+                row_ring(moves, rank, 1, piece, halves, dz, got[dz], late)
+        else:
+            got = row_ring(moves, rank, 0, piece, halves, 0, [], 0)
+            for late, dy in enumerate((0, -1, 1, 2)):
+                column_ring(moves, rank, 1 + late, piece, halves, dy, got[dy])
+    return moves
+
+
+def gather_program(moves, depth, rate=46.5e3, latency=1.7):
+    issued, got = set(), set()
+    free, flying = dict.fromkeys(LINKS, 0.0), dict.fromkeys(LINKS, 0)
+    arrivals, now, program = [], 0.0, []
+    while True:
+        for link in LINKS:
+            while flying[link] < depth:
+                ready = [
+                    (moves[i][4], i)
+                    for i in range(len(moves))
+                    if moves[i][0] == link and i not in issued and got.issuperset(moves[i][3])
+                ]
+                if not ready:
+                    break
+                i = min(ready)[1]
+                _, r0, r1, c0, c1 = moves[i][2]
+                issued.add(i)
+                flying[link] += 1
+                program.append(("send", i, now))
+                free[link] = max(now, free[link]) + (r1 - r0) * (c1 - c0) * 2 / rate
+                heapq.heappush(arrivals, (free[link] + latency, i))
+        if not arrivals:
+            return program
+        now, i = heapq.heappop(arrivals)
+        got.add(i)
+        flying[moves[i][0]] -= 1
+        program.append(("recv", i, now))
+
+
+PIECES = (
+    (0, "zy", ("gu", 0, 96, 0, 1536), (("gu", 0, 48, 0, 1536), ("gu", 48, 96, 0, 1536))),
+    (0, "yz", ("dn", 0, 48, 0, 1536), (("dn", 0, 48, 0, 768), ("dn", 0, 48, 768, 1536))),
+)
+
+
+def gather_kernel(moves, program, gu_own, dn_own, gu_all, dn_all, own_sem, send_sem, recv_sem):
+    dp, mp, expert = (lax.axis_index(a) for a in AXES)
+    y, z_lo, z_hi, core = dp // 4, dp % 4, expert // 2, expert % 2
+    z = z_hi * 4 + z_lo
+
+    def place(dy, dz):
+        other_y, other_z = (y + dy + 8) % 4, (z + dz + 8) % 8
+        return other_z // 4, other_y * 4 + other_z % 4
+
+    def device(dy, dz):
+        half, index = place(dy, dz)
+        return (index, mp, half * 2 + core)
+
+    target = {"y+": (1, 0), "y-": (-1, 0), "z+": (0, 1), "z-": (0, -1)}
+    own, whole = {"gu": gu_own, "dn": dn_own}, {"gu": gu_all, "dn": dn_all}
+
+    barrier = pltpu.get_barrier_semaphore()
+    for link in LINKS:
+        pl.semaphore_signal(barrier, inc=1, device_id=device(*target[link]), device_id_type=MESH)
+    pl.semaphore_wait(barrier, 4)
+
+    def copy(i):
+        link, (dy, dz), (name, r0, r1, c0, c1), _, _ = moves[i]
+        half, index = place(dy, dz)
+        rows, columns = pl.ds(r0, r1 - r0), pl.ds(c0, c1 - c0)
+        landing = whole[name].at[half, index, rows, columns]
+        start = own[name].at[rows, columns] if (dy, dz) == (0, 0) else landing
+        return pltpu.make_async_remote_copy(
+            src_ref=start,
+            dst_ref=landing,
+            send_sem=send_sem.at[i],
+            recv_sem=recv_sem.at[i],
+            device_id=device(*target[link]),
+            device_id_type=MESH,
+        )
+
+    half, index = place(0, 0)
+    kept = [
+        pltpu.make_async_copy(own[name], whole[name].at[half, index], own_sem.at[k])
+        for k, name in enumerate(("gu", "dn"))
+    ]
+    for c in kept:
+        c.start()
+    for kind, i, _ in program:
+        if kind == "send":
+            copy(i).start()
+        else:
+            copy(i).wait_recv()
+    for i in range(len(moves)):
+        copy(i).wait_send()
+    for c in kept:
+        c.wait()
+
+
+def gather_weights(gateup, down):
+    moves = gather_moves(PIECES)
+    program = gather_program(moves, 4)
+    return pl.pallas_call(
+        functools.partial(gather_kernel, moves, program),
+        out_shape=[
+            jax.ShapeDtypeStruct((2, 16) + gateup.shape, jnp.bfloat16),
+            jax.ShapeDtypeStruct((2, 16) + down.shape, jnp.bfloat16),
+        ],
+        in_specs=[pl.BlockSpec(memory_space=pl.ANY)] * 2,
+        out_specs=[pl.BlockSpec(memory_space=pl.ANY)] * 2,
+        scratch_shapes=[
+            pltpu.SemaphoreType.DMA((2,)),
+            pltpu.SemaphoreType.DMA((len(moves),)),
+            pltpu.SemaphoreType.DMA((len(moves),)),
+        ],
+        compiler_params=pltpu.CompilerParams(collective_id=0, has_side_effects=True),
+    )(gateup, down)
 
 
 def shifted(value, axis, steps):
@@ -48,9 +203,13 @@
     routes,
     route_weights,
 ):
+    both_gateup, both_down = gather_weights(
+        trainer_gateup[0].astype(jnp.bfloat16), trainer_down[0].astype(jnp.bfloat16)
+    )
+    half = lax.axis_index("expert") // 2
     gateup_full, down_full = (
-        lax.all_gather(trainer_gateup.astype(jnp.bfloat16), "dp", axis=1, tiled=True),
-        lax.all_gather(trainer_down.astype(jnp.bfloat16), "dp", axis=1, tiled=True),
+        lax.dynamic_index_in_dim(both, half, 0, keepdims=True).reshape(1, -1, MODEL_WIDTH)
+        for both in (both_gateup, both_down)
     )
     own_rows = tokens.shape[0]
     head_group_index = lax.axis_index(("dp", "expert"))

time: 397 us -> 335 us (0.84)
  waiting for transfers between devices: 289 us -> 88.8 us
  Pallas kernels: 0 us -> 134 us
  local copies, waits for them, and re-layouts: 24.8 us -> 33 us
  matrix products: 24.6 us -> 18.9 us
  starting transfers between devices: 27.1 us -> 31.9 us
    pallas_call x0 -> x1, Pallas kernels: none -> 134 us  [gather_weights(): pl.pallas_call(functools.partial(gather_kernel, moves, program), out_shap...]
    all_to_all x1, waiting for transfers between devices: 110 us -> 0.01 us  [body(): lax.all_to_all(buffer, ('mp', 'expert'), split_axis=0, concat_axis=0, til...]
    all_gather x2 -> x0, waiting for transfers between devices: 91.5 us -> none  [the longest x1 82.1 us: body(): lax.all_gather(trainer_down.astype(jnp.bfloat16), 'dp', axis=1, tiled=True)]
    dynamic_slice x0 -> x2, local copies, waits for them, and re-layouts: none -> 8.21 us  [body(): lax.dynamic_index_in_dim(both, half, 0, keepdims=True)]
    ppermute x3, waiting for transfers between devices: 9.36 us -> 1.49 us  [shifted(): lax.ppermute(value, axis, [(source, source + steps) for source in range(i...]
    reduce_scatter x1, waiting for transfers between devices: 21.6 us -> 28.7 us  [body(): lax.psum_scatter(jnp.dot(attended, output_weight, preferred_element_type=...]
    ppermute x3, starting transfers between devices: 12.9 us -> 17 us  [shifted(): lax.ppermute(value, axis, [(source, source + steps) for source in range(i...]
  transfers between devices with their start and end apart: 8 -> 6, of which waited for: 7 -> 3; matrix products, arithmetic and copies ran while one was open for 8% -> 7% of each run, Pallas kernels for 0% -> 40%
where the time goes in v1:
time: 335 us; the launch traced here: 334 us
  Pallas kernels  134 us (40%)
  waiting for transfers between devices  88.8 us (27%)
  local copies, waits for them, and re-layouts  33 us (10%)
  starting transfers between devices  31.9 us (10%)
  matrix products  18.9 us (6%)
  other arithmetic  14 us (4%)
  between operations  13.7 us (4%)
    pallas_call x1, Pallas kernels, gather_weights(): pl.pallas_call(functools.partial(gather_kernel, moves, program), out_shap...  134 us
    all_to_all x1, waiting for transfers between devices, body(): lax.all_to_all(produced, ('mp', 'expert'), split_axis=0, concat_axis=0, t...  58.6 us
    reduce_scatter x1, waiting for transfers between devices, body(): lax.psum_scatter(jnp.dot(attended, output_weight, preferred_element_type=...  28.7 us
    ppermute x3, starting transfers between devices, shifted(): lax.ppermute(value, axis, [(source, source + steps) for source in range(i...  17 us
    gather x1, local copies, waits for them, and re-layouts, body(): key_segment = jnp.where(key_pos >= 0, segments[jnp.maximum(key_pos, 0)], -1)  8.38 us
    dynamic_slice x2, local copies, waits for them, and re-layouts, body(): lax.dynamic_index_in_dim(both, half, 0, keepdims=True)  8.21 us
    all_to_all x1, starting transfers between devices, body(): lax.all_to_all(produced, ('mp', 'expert'), split_axis=0, concat_axis=0, t...  7.67 us
    all_to_all x1, starting transfers between devices, body(): lax.all_to_all(buffer, ('mp', 'expert'), split_axis=0, concat_axis=0, til...  7.29 us
  transfers between devices with their start and end apart: 6, of which 3 were waited for; matrix products, arithmetic and copies ran while one was open for 7% of the time, Pallas kernels for 40%

profile of v1, /device:TPU:32, one launch (start us, length us, event | category | flops | bytes accessed | tf_op | source)
XLA Modules:
  0.0 333.9 jit_solution(7775399743113715891)
XLA Ops:
  6.5 0.0 copy-start
  6.5 0.0 copy-start.1
  6.5 0.0 reduce-scatter.2.cloned.1.call-start
  6.5 0.9 slice_reduce_fusion.1
  7.4 1.6 fusion.8
  9.0 0.0 copy-done
  9.0 1.8 convolution_convert_fusion.3
  10.8 1.9 collective-permute-start.2
  12.8 8.2 %collective-permute-start.1 = (bf16[384,256]{1,0:T(8,128)(2,1)S(1)}, bf16[384,256]{1,0:T(8,128)(2,1)S(1)}, u32[]{:S(2)}, u32[]{:S(2)}) collective-permute-start(bf16[384,256]{1,0:T(8,128)(2,1)S(1)} %convolution_convert_fusion.3), channel_id=1, source_target_pairs={{0,2},{1,3},{2,16},{3,17},{16,18},{17,19},{18,32},{19,33},{32,34},... | collective-permute-start | bytes 589832 | tf_op jit(solution)/shard_map/ppermute | solution.py:175
  21.0 6.8 %collective-permute-start = (bf16[384,256]{1,0:T(8,128)(2,1)S(1)}, bf16[384,256]{1,0:T(8,128)(2,1)}, u32[]{:S(2)}, u32[]{:S(2)}) collective-permute-start(bf16[384,256]{1,0:T(8,128)(2,1)S(1)} %convolution_convert_fusion.3), channel_id=1, source_target_pairs={{0,3},{1,16},{2,17},{3,18},{16,19},{17,32},{18,33},{19,34},{32,35}... | collective-permute-start | bytes 589832 | tf_op jit(solution)/shard_map/ppermute | solution.py:175
  27.9 0.0 copy-done.1
  27.9 0.1 dynamic_slice.25
  28.0 0.0 copy-start.3
  28.0 8.4 %gather_fusion = s32[1536]{0:T(1024)S(1)} fusion(s32[24576]{0:T(1024)S(1)} %copy-done.1, s32[2048]{0:T(1024)S(1)} %pad_clamp_fusion), kind=kCustom, calls=%fused_computation | custom fusion | bytes 18432 | tf_op jit(solution)/shard_map/gather | solution.py:245
  36.4 1.1 compare_and_fusion
  37.5 0.0 copy-done.3
  37.5 2.2 convolution_convert_fusion.2
  39.7 0.0 collective-permute-done.2
  39.7 1.5 collective-permute-done.1
  41.2 0.0 collective-permute-done
  41.2 1.0 pad_maximum_fusion
  42.1 1.5 fusion
  43.7 1.5 fusion.3
  45.3 0.0 copy-start.4
  45.3 1.7 fusion.22
  47.0 0.0 copy-done.4
  47.0 1.8 convolution_convert_fusion.1
  48.8 0.0 reduce-scatter.2.cloned.1.call-update
  48.8 0.8 broadcast_multiply_fusion
  49.6 0.1 copy.20
  49.7 0.1 eq.45
  49.8 0.1 eq.49
  49.9 0.1 copy.19
  50.0 0.1 mul.97
  50.1 0.9 reduce-window.6
  51.0 0.2 slice_reduce_fusion
  51.2 0.1 fusion.37
  51.4 28.7 %reduce-scatter.2.cloned.1.call-done = bf16[96,1536]{1,0:T(8,128)(2,1)} async-done(((bf16[384,1536]{1,0:T(8,128)(2,1)}), bf16[96,1536]{1,0:T(8,128)(2,1)}) %reduce-scatter.2.cloned.1.call-update) | async-done | bytes 294928 | tf_op jit(solution)/shard_map/reduce_scatter | solution.py:274
  80.0 1.2 fusion.27
  81.2 0.1 fusion.29
  81.4 0.3 broadcast_in_dim.51
  81.7 1.2 reshape.202
  82.9 4.8 %scatter_custom_fusion = bf16[768,1536]{1,0:T(8,128)(2,1)} fusion(s32[384]{0:T(512)S(1)} %fusion.39, bf16[384,1536]{1,0:T(8,128)(2,1)} %reshape.202, bf16[]{:T(256)} %constant.91.clone.1), kind=kCustom, calls=%fused_computation.27 | custom fusion | bytes 2359808 | tf_op jit(solution)/shard_map/scatter | solution.py:294
  87.7 0.0 copy-start.6
  87.7 7.3 %all-to-all-start = ((bf16[16,48,1536]{2,1,0:T(8,128)(2,1)}), bf16[16,48,1536]{2,1,0:T(8,128)(2,1)}, u32[]{:S(2)}, u32[]{:S(2)}) async-start(bf16[16,48,1536]{2,1,0:T(8,128)(2,1)} %bitcast.79), calls=%async_computation.1 | async-start | bytes 4718592 | tf_op jit(solution)/shard_map/all_to_all | solution.py:297
  95.0 0.0 copy-done.6
  95.0 0.7 convert_bitcast_fusion.1.dn_own
  95.7 0.0 copy-done.5
  95.7 0.7 convert_bitcast_fusion.gu_own
  96.4 133.6 %shard_map.100 = (bf16[2,16,96,1536]{3,2,1,0:T(8,128)(2,1)}, bf16[2,16,48,1536]{3,2,1,0:T(8,128)(2,1)}) custom-call(bf16[96,1536]{1,0:T(8,128)(2,1)} %convert_bitcast_fusion.gu_own, bf16[48,1536]{1,0:T(8,128)(2,1)} %convert_bitcast_fusion.1.dn_own), custom_call_target="tpu_custom_call" | custom-call | tf_op jit(solution)/shard_map/pallas_call | solution.py:155
  230.1 3.2 constant_dynamic-slice_fusion
  233.3 5.0 %constant_dynamic-slice_fusion.1 = bf16[1,16,96,1536]{3,2,1,0:T(8,128)(2,1)} fusion(bf16[2,16,96,1536]{3,2,1,0:T(8,128)(2,1)} %get-tuple-element.7, s32[]{:T(128)S(6)} %select_n.62), kind=kLoop, calls=%fused_computation.71 | loop fusion | bytes 9437188 | tf_op jit(solution)/shard_map/jit(dynamic_index_in_dim)/dynamic_slice | solution.py:211
  238.3 0.0 all-to-all-done
  238.3 6.5 %fusion.44 = f32[768,1536]{1,0:T(8,128)S(1)} fusion(bf16[768,1536]{1,0:T(8,128)(2,1)} %bitcast.10, bf16[1536,1536]{1,0:T(8,128)(2,1)} %bitcast.80), kind=kOutput, calls=%fused_computation.80 | convolution fusion | flops 3623878656 | bytes 11796480 | tf_op jit(solution)/shard_map/dot_general | solution.py:300
  244.8 0.0 copy-done.2
  244.8 3.4 %convolution_convert_fusion = bf16[768,1536]{1,0:T(8,128)(2,1)} fusion(bf16[768,1536]{1,0:T(8,128)(2,1)S(1)} %bitcast.81, f32[768,1536]{1,0:T(8,128)S(1)} %fusion.44), kind=kOutput, calls=%fused_computation.12 | convolution fusion | flops 1814888448 | bytes 9437184 | tf_op jit(solution)/shard_map/dot_general | solution.py:307
  248.2 7.7 %all-to-all-start.1 = ((bf16[16,48,1536]{2,1,0:T(8,128)(2,1)}), bf16[16,48,1536]{2,1,0:T(8,128)(2,1)}, u32[]{:S(2)}, u32[]{:S(2)}) async-start(bf16[16,48,1536]{2,1,0:T(8,128)(2,1)} %bitcast.82), calls=%async_computation.2 | async-start | bytes 4718592 | tf_op jit(solution)/shard_map/all_to_all | solution.py:311
  255.9 0.8 constant_dynamic-slice_fusion.3
  256.7 0.1 copy.18
  256.8 58.6 %all-to-all-done.1 = bf16[16,48,1536]{2,1,0:T(8,128)(2,1)} async-done(((bf16[16,48,1536]{2,1,0:T(8,128)(2,1)}), bf16[16,48,1536]{2,1,0:T(8,128)(2,1)}, u32[]{:S(2)}, u32[]{:S(2)}) %all-to-all-start.1) | async-done | bytes 2359328 | tf_op jit(solution)/shard_map/all_to_all | solution.py:311
  315.4 5.7 %gather_fusion.1 = bf16[384,1536]{1,0:T(8,128)(2,1)S(1)} fusion(bf16[768,1536]{1,0:T(8,128)(2,1)} %bitcast.16, s32[1024]{0:T(1024)S(1)} %pad_clamp_fusion.1), kind=kCustom, calls=%fused_computation.1 | custom fusion | bytes 2360832 | tf_op jit(solution)/shard_map/gather | solution.py:313
  321.1 1.8 reshape.181
  322.9 3.4 %multiply_reduce_fusion = f32[96,1536]{1,0:T(8,128)S(1)} fusion(f32[96,4,1536]{2,1,0:T(4,128)} %reshape.181, f32[96,4]{1,0:T(8,128)S(1)} %copy.18), kind=kLoop, calls=%fused_computation.22 | loop fusion | flops 1032192 | bytes 2950656 | tf_op jit(solution)/shard_map/reduce_sum | solution.py:317
  326.3 0.8 fusion.34
  (13 shorter events, 0.1 us)
Async XLA Ops:
  6.5 2.5 copy-start
  6.5 21.4 %copy-start.1 = (s32[24576]{0:T(1024)S(1)}, s32[24576]{0:T(1024)}, u32[]{:S(2)}) copy-start(s32[24576]{0:T(1024)} %param.11) | copy-start | bytes 294916
  6.5 73.5 %reduce-scatter.2.cloned.1.call-start = ((), (), s32[]{:S(2)}) async-start(), calls=%async_computation.3 | async-start | bytes 1474560 | tf_op jit(solution)/shard_map/reduce_scatter | solution.py:274
  10.8 28.8 %collective-permute-start.2 = (bf16[384,256]{1,0:T(8,128)(2,1)S(1)}, bf16[384,256]{1,0:T(8,128)(2,1)S(1)}, u32[]{:S(2)}, u32[]{:S(2)}) collective-permute-start(bf16[384,256]{1,0:T(8,128)(2,1)S(1)} %convolution_convert_fusion.3), channel_id=1, source_target_pairs={{0,1},{1,2},{2,3},{3,16},{16,17},{17,18},{18,19},{19,32},{32,33},{... | collective-permute-start | bytes 589832 | tf_op jit(solution)/shard_map/ppermute | solution.py:175
  12.8 28.4 %collective-permute-start.1 = (bf16[384,256]{1,0:T(8,128)(2,1)S(1)}, bf16[384,256]{1,0:T(8,128)(2,1)S(1)}, u32[]{:S(2)}, u32[]{:S(2)}) collective-permute-start(bf16[384,256]{1,0:T(8,128)(2,1)S(1)} %convolution_convert_fusion.3), channel_id=1, source_target_pairs={{0,2},{1,3},{2,16},{3,17},{16,18},{17,19},{18,32},{19,33},{32,34},... | collective-permute-start | bytes 589832 | tf_op jit(solution)/shard_map/ppermute | solution.py:175
  21.0 20.2 %collective-permute-start = (bf16[384,256]{1,0:T(8,128)(2,1)S(1)}, bf16[384,256]{1,0:T(8,128)(2,1)}, u32[]{:S(2)}, u32[]{:S(2)}) collective-permute-start(bf16[384,256]{1,0:T(8,128)(2,1)S(1)} %convolution_convert_fusion.3), channel_id=1, source_target_pairs={{0,3},{1,16},{2,17},{3,18},{16,19},{17,32},{18,33},{19,34},{32,35}... | collective-permute-start | bytes 589832 | tf_op jit(solution)/shard_map/ppermute | solution.py:175
  28.0 9.5 %copy-start.3 = (bf16[384,1536]{1,0:T(8,128)(2,1)S(1)}, bf16[384,1536]{1,0:T(8,128)(2,1)}, u32[]{:S(2)}) copy-start(bf16[384,1536]{1,0:T(8,128)(2,1)} %param.10) | copy-start | bytes 3538948
  45.3 1.7 copy-start.4
  87.7 7.3 %copy-start.6 = (f32[1,48,1536]{2,1,0:T(8,128)S(1)}, f32[1,48,1536]{2,1,0:T(8,128)}, u32[]{:S(2)}) copy-start(f32[1,48,1536]{2,1,0:T(8,128)} %param.17) | copy-start | bytes 884740
  87.7 8.0 %copy-start.5 = (f32[1,96,1536]{2,1,0:T(8,128)S(1)}, f32[1,96,1536]{2,1,0:T(8,128)}, u32[]{:S(2)}) copy-start(f32[1,96,1536]{2,1,0:T(8,128)} %param.16) | copy-start | bytes 1769476
  87.7 150.6 %all-to-all-start = ((bf16[16,48,1536]{2,1,0:T(8,128)(2,1)}), bf16[16,48,1536]{2,1,0:T(8,128)(2,1)}, u32[]{:S(2)}, u32[]{:S(2)}) async-start(bf16[16,48,1536]{2,1,0:T(8,128)(2,1)} %bitcast.79), calls=%async_computation.1 | async-start | bytes 4718592 | tf_op jit(solution)/shard_map/all_to_all | solution.py:297
  238.3 6.6 %copy-start.2 = (bf16[1,16,48,1536]{3,2,1,0:T(8,128)(2,1)S(1)}, bf16[1,16,48,1536]{3,2,1,0:T(8,128)(2,1)}, u32[]{:S(2)}) copy-start(bf16[1,16,48,1536]{3,2,1,0:T(8,128)(2,1)} %constant_dynamic-slice_fusion) | copy-start | bytes 7077892
  248.2 67.2 %all-to-all-start.1 = ((bf16[16,48,1536]{2,1,0:T(8,128)(2,1)}), bf16[16,48,1536]{2,1,0:T(8,128)(2,1)}, u32[]{:S(2)}, u32[]{:S(2)}) async-start(bf16[16,48,1536]{2,1,0:T(8,128)(2,1)} %bitcast.82), calls=%async_computation.2 | async-start | bytes 4718592 | tf_op jit(solution)/shard_map/all_to_all | solution.py:311
Sparse Core Ops, SparseCore 0:
  48.9 31.0 reduce-scatter.1

commit v2 on v1

v2 whole, which is shorter than its diff:
```python
import functools
import heapq
import math
import types

import jax
import jax.numpy as jnp
from jax import lax
from jax.experimental import pallas as pl
from jax.experimental.pallas import tpu as pltpu
from jax.sharding import PartitionSpec as P

MODEL_WIDTH = 1536
FF = 768
TOPK = 4


LINKS = ("y+", "y-", "z+", "z-")
AXES = ("dp", "mp", "expert")
MESH = pl.DeviceIdType.MESH


def column_ring(moves, rank, tag, piece, halves, dy, have):
    got = {0: have}
    up, down = have, have
    for s in range(1, 4):
        moves.append(("z+", (dy, 1 - s), piece, up, (rank, tag, s)))
        up = got[-s] = [len(moves) - 1]
        moves.append(("z-", (dy, s - 1), piece, down, (rank, tag, s)))
        down = got[s] = [len(moves) - 1]
    moves.append(("z+", (dy, -3), halves[0], up, (rank, tag, 4)))
    moves.append(("z-", (dy, 3), halves[1], down, (rank, tag, 4)))
    got[4] = [len(moves) - 2, len(moves) - 1]
    return got


def row_ring(moves, rank, tag, piece, halves, dz, have, late):
    start = len(moves)
    moves.append(("y+", (0, dz), piece, have, (rank, tag, 1 + late)))
    moves.append(("y-", (0, dz), piece, have, (rank, tag, 1 + late)))
    moves.append(("y+", (-1, dz), halves[0], [start], (rank, tag, 2 + late)))
    moves.append(("y-", (1, dz), halves[1], [start + 1], (rank, tag, 2 + late)))
    return {0: have, -1: [start], 1: [start + 1], 2: [start + 2, start + 3]}


def gather_moves(pieces):
    moves = []
    for rank, order, piece, halves in pieces:
        if order == "zy":
            got = column_ring(moves, rank, 0, piece, halves, 0, [])
            for late, dz in enumerate((0, -1, 1, -2, 2, -3, 3, 4)):
                row_ring(moves, rank, 1, piece, halves, dz, got[dz], late)
        else:
            got = row_ring(moves, rank, 0, piece, halves, 0, [], 0)
            for late, dy in enumerate((0, -1, 1, 2)):
                column_ring(moves, rank, 1 + late, piece, halves, dy, got[dy])
    return moves


def gather_program(moves, depth, rate=46.5e3, latency=1.7):
    issued, got = set(), set()
    free, flying = dict.fromkeys(LINKS, 0.0), dict.fromkeys(LINKS, 0)
    arrivals, now, program = [], 0.0, []
    while True:
        for link in LINKS:
            while flying[link] < depth:
                ready = [
                    (moves[i][4], i)
                    for i in range(len(moves))
                    if moves[i][0] == link and i not in issued and got.issuperset(moves[i][3])
                ]
                if not ready:
                    break
                i = min(ready)[1]
                _, r0, r1, c0, c1 = moves[i][2]
                issued.add(i)
                flying[link] += 1
                program.append(("send", i, now))
                free[link] = max(now, free[link]) + (r1 - r0) * (c1 - c0) * 2 / rate
                heapq.heappush(arrivals, (free[link] + latency, i))
        if not arrivals:
            return program
        now, i = heapq.heappop(arrivals)
        got.add(i)
        flying[moves[i][0]] -= 1
        program.append(("recv", i, now))


PIECES = (
    (0, "zy", ("gu", 0, 96, 0, 1024), (("gu", 0, 48, 0, 1024), ("gu", 48, 96, 0, 1024))),
    (0, "yz", ("gu", 0, 96, 1024, 1536), (("gu", 0, 48, 1024, 1536), ("gu", 48, 96, 1024, 1536))),
    (1, "zy", ("dn", 0, 48, 0, 768), (("dn", 0, 48, 0, 384), ("dn", 0, 48, 384, 768))),
    (1, "yz", ("dn", 0, 48, 768, 1536), (("dn", 0, 48, 768, 1152), ("dn", 0, 48, 1152, 1536))),
)
DEPTH = 6
PUMP = dict(
    start=0.1, kv=4, query=8, attend=(14, 16, 18), project=22, middle=34, dispatch=44,
    gather=(46, 47, 48, 49), gate=(54, 57, 60, 63, 66, 69),
)

ROWS = 384
PART = 96
SLOTS = 48
WINDOW = 1152
F_CHUNK = 256
N_CHUNK = 512
N_CHUNKS = MODEL_WIDTH // N_CHUNK


def dot(a, b):
    return jnp.dot(a, b, preferred_element_type=jnp.float32)


def layer_kernel(moves, program, refs):
    r = refs
    dp, mp, expert = (lax.axis_index(a) for a in AXES)
    y, z_lo, z_hi, core = dp // 4, dp % 4, expert // 2, expert % 2
    z = z_hi * 4 + z_lo
    group = dp * 4 + expert

    def place(dy, dz):
        other_y, other_z = (y + dy + 8) % 4, (z + dz + 8) % 8
        return other_z // 4, other_y * 4 + other_z % 4

    def grid_device(dy, dz):
        half, index = place(dy, dz)
        return (index, mp, half * 2 + core)

    def column_device(d):
        return (dp, (mp + d + 4) % 4, expert)

    def piece_device(d):
        other = (group + d + 64) % 64
        return (other // 4, mp, other % 4)

    partner = (dp, mp, z_hi * 2 + 1 - core)
    target = {"y+": (1, 0), "y-": (-1, 0), "z+": (0, 1), "z-": (0, -1)}

    barrier = pltpu.get_barrier_semaphore()
    greeted = [grid_device(*target[link]) for link in LINKS]
    greeted += [column_device(d) for d in (1, 2, 3)] + [piece_device(-d) for d in (1, 2, 3)]
    greeted.append(partner)
    for other in greeted:
        pl.semaphore_signal(barrier, inc=1, device_id=other, device_id_type=MESH)
    pl.semaphore_wait(barrier, len(greeted))

    def remote(start, landing, sems, i, device):
        return pltpu.make_async_remote_copy(
            src_ref=start,
            dst_ref=landing,
            send_sem=sems[0].at[i],
            recv_sem=sems[1].at[i],
            device_id=device,
            device_id_type=MESH,
        )

    own, whole = {"gu": r.gu_own, "dn": r.dn_own}, {"gu": r.gu, "dn": r.dn}

    def weight_copy(i):
        link, (dy, dz), (name, r0, r1, c0, c1), _, _ = moves[i]
        half, index = place(dy, dz)
        rows, columns = pl.ds(r0, r1 - r0), pl.ds(c0, c1 - c0)
        landing = whole[name].at[half, index, rows, columns]
        start = own[name].at[rows, columns] if (dy, dz) == (0, 0) else landing
        return remote(start, landing, r.weight_sems, i, grid_device(*target[link]))

    position = [0]

    def pump(until=None, needed=None):
        while position[0] < len(program):
            kind, i, when = program[position[0]]
            if until is not None and when > until:
                return
            if kind == "send":
                weight_copy(i).start()
            else:
                weight_copy(i).wait_recv()
                if needed is not None:
                    needed.discard(i)
            position[0] += 1
            if needed is not None and not needed:
                return

    half, index = place(0, 0)
    kept = [
        pltpu.make_async_copy(own[name], whole[name].at[half, index], r.own_sems.at[k])
        for k, name in enumerate(("gu", "dn"))
    ]
    for c in kept:
        c.start()
    routing = remote(r.routing, r.routing_other, r.routing_sems, 0, partner)
    routing.start()
    pump(PUMP["start"])

    gain = r.gains[0:1, :]

    @pl.loop(0, ROWS // 32)
    def _(i):
        rows = pl.ds(pl.multiple_of(i * 32, 32), 32)
        wide = r.tokens[rows, :].astype(jnp.float32)
        scale = lax.rsqrt(jnp.mean(wide * wide, axis=-1, keepdims=True) + 1e-6)
        r.normed[rows, :] = (wide * scale * gain).astype(jnp.bfloat16)

    r.pairs[WINDOW:, :] = dot(r.normed[...], r.pair_weight[mp // 2]).astype(jnp.bfloat16)

    def pair_copy(d):
        first = 128 if d == 3 else 0
        rows = ROWS - first
        return remote(
            r.pairs.at[pl.ds(WINDOW + first, rows), :],
            r.pairs.at[pl.ds(WINDOW - d * ROWS + first, rows), :],
            r.pair_sems,
            d - 1,
            piece_device(d),
        )

    for d in (1, 2, 3):
        pair_copy(d).start()
    pump(PUMP["kv"])
    r.queries[...] = dot(r.normed[...], r.query_weight[...]).astype(jnp.bfloat16)
    pump(PUMP["query"])

    lanes = []
    for k in range(12):
        row = (group * 3 - 9 + k + 192) % 192
        lanes.append(r.segments[pl.ds(row, 1), :])
    key_segment = jnp.concatenate(lanes, axis=1)
    diagonal = lax.broadcasted_iota(jnp.int32, (128, 128), 0) == lax.broadcasted_iota(
        jnp.int32, (128, 128), 1
    )
    first_key = (group - 3) * ROWS

    for d in (1, 2, 3):
        pair_copy(d).wait_recv()
    for c in range(3):
        low = (c + 1) * 128
        own_lanes = jnp.broadcast_to(lanes[9 + c].astype(jnp.float32), (128, 128))
        query_segment = jnp.sum(jnp.where(diagonal, own_lanes, 0.0), axis=1, keepdims=True)
        key_offset = low + lax.broadcasted_iota(jnp.int32, (128, WINDOW), 1)
        query_offset = WINDOW + c * 128 + lax.broadcasted_iota(jnp.int32, (128, WINDOW), 0)
        allowed = (
            (key_segment[:, low : low + WINDOW].astype(jnp.float32) == query_segment)
            & (key_offset <= query_offset)
            & (key_offset + first_key >= 0)
        )
        keys = r.pairs[low : low + WINDOW, :128]
        values = r.pairs[low : low + WINDOW, 128:]
        for h in range(3):
            query = r.queries[c * 128 : (c + 1) * 128, h * 128 : (h + 1) * 128]
            scores = lax.dot_general(
                query, keys, (((1,), (1,)), ((), ())), preferred_element_type=jnp.float32
            )
            scores = jnp.where(allowed, scores * (1.0 / math.sqrt(128)), -1e30)
            weights = jnp.exp(scores - jnp.max(scores, axis=1, keepdims=True))
            total = jnp.sum(weights, axis=1, keepdims=True)
            mixed = dot(weights.astype(jnp.bfloat16), values) / total
            r.attended[c * 128 : (c + 1) * 128, h * 128 : (h + 1) * 128] = mixed.astype(jnp.bfloat16)
        pump(PUMP["attend"][c])

    def partial_copy(d):
        return remote(
            r.projected.at[(mp + d) % 4], r.projected_in.at[d - 1], r.projected_sems, d - 1, column_device(d)
        )

    r.projected[...] = (
        dot(r.attended[...], r.output_weight[...]).astype(jnp.bfloat16).reshape(4, PART, MODEL_WIDTH)
    )
    pump(PUMP["project"])
    for d in (2, 1, 3):
        partial_copy(d).start()

    routing.wait_recv()
    earlier = (
        lax.broadcasted_iota(jnp.int32, (PART, PART), 0) < lax.broadcasted_iota(jnp.int32, (PART, PART), 1)
    ).astype(jnp.bfloat16)
    slot = lax.broadcasted_iota(jnp.int32, (SLOTS, PART), 0).astype(jnp.float32)
    served = [(mp * 4 + e * 2 + core).astype(jnp.float32) for e in range(2)]
    for d in range(4):
        m = (mp - d + 4) % 4
        for side, table in enumerate((r.routing, r.routing_other)):
            routes, gates = table[m, 0:4, :], table[m, 4:8, :]
            for e in range(2):
                named = routes == served[e]
                hit = jnp.sum(jnp.where(named, 1.0, 0.0), axis=0, keepdims=True)
                gate = jnp.sum(jnp.where(named, gates, 0.0), axis=0, keepdims=True)
                rank = dot(jnp.broadcast_to(hit, (8, PART)).astype(jnp.bfloat16), earlier)[0:1, :]
                chosen = jnp.where((slot == rank) & (hit > 0.5), 1.0, 0.0)
                r.slots[d, side, e * SLOTS : (e + 1) * SLOTS, :] = chosen.astype(jnp.bfloat16)
                r.slot_gates[e, d, side * SLOTS : (side + 1) * SLOTS, :] = jnp.sum(
                    chosen * gate, axis=1, keepdims=True
                )
    pump(PUMP["middle"])

    for d in (1, 2, 3):
        partial_copy(d).wait_recv()
    summed = r.tokens[pl.ds(pl.multiple_of(mp * PART, PART), PART), :].astype(jnp.float32)
    attention = r.projected[mp].astype(jnp.float32)
    for d in range(3):
        attention = attention + r.projected_in[d].astype(jnp.float32)
    middle = (summed + attention).astype(jnp.bfloat16)
    r.middle[...] = middle
    wide = middle.astype(jnp.float32)
    scale = lax.rsqrt(jnp.mean(wide * wide, axis=-1, keepdims=True) + 1e-6)
    r.states[0, 0] = (wide * scale * r.gains[1:2, :]).astype(jnp.bfloat16)

    def state_copy(d):
        return remote(r.states.at[0, 0], r.states.at[0, d], r.state_sems, d - 1, column_device(d))

    def across_copy(d):
        return remote(r.states.at[0, d], r.states.at[1, d], r.across_sems, d, partner)

    for d in (2, 1, 3):
        state_copy(d).start()
    across_copy(0).start()
    pump(PUMP["dispatch"])
    for step, d in enumerate((0, 1, 3, 2)):
        if d:
            state_copy(d).wait_recv()
            across_copy(d).start()
        for side in range(2):
            if side:
                across_copy(d).wait_recv()
            picked = dot(r.slots[d, side], r.states[side, d]).astype(jnp.bfloat16)
            for e in range(2):
                r.routed[e, d, side * SLOTS : (side + 1) * SLOTS, :] = picked[e * SLOTS : (e + 1) * SLOTS]
        pump(PUMP["gather"][step])

    for k in range(2):
        kept[k].wait()
    arrived = {i for kind, i, _ in program[: position[0]] if kind == "recv"}
    missing = {i for i, move in enumerate(moves) if move[2][0] == "gu"} - arrived
    if missing:
        pump(needed=missing)
    for e in range(2):
        inputs = r.routed[e].reshape(4 * PART, MODEL_WIDTH)
        for f in range(3):
            left = f * F_CHUNK
            gate = dot(inputs, r.gu[e, :, :, left : left + F_CHUNK].reshape(MODEL_WIDTH, F_CHUNK))
            rise = dot(inputs, r.gu[e, :, :, FF + left : FF + left + F_CHUNK].reshape(MODEL_WIDTH, F_CHUNK))
            r.hidden[e, :, left : left + F_CHUNK] = (jnp.maximum(gate, 0.0) * rise).astype(jnp.bfloat16)
            pump(PUMP["gate"][e * 3 + f])
    pump()

    def return_core(n):
        columns = pl.ds(n * N_CHUNK, N_CHUNK)
        return remote(
            r.outgoing.at[1, :, :, columns], r.core_in.at[:, :, columns], r.core_sems, n, partner
        )

    def return_column(n, d):
        columns = pl.ds(n * N_CHUNK, N_CHUNK)
        return remote(
            r.merged.at[d, :, columns],
            r.column_in.at[d - 1, :, columns],
            r.column_sems,
            n * 3 + d - 1,
            column_device(-d),
        )

    def merge(n):
        columns = slice(n * N_CHUNK, (n + 1) * N_CHUNK)
        return_core(n).wait_recv()
        for d in (2, 1, 3, 0):
            both = r.outgoing[0, d, :, columns].astype(jnp.float32) + r.core_in[d, :, columns].astype(
                jnp.float32
            )
            r.merged[d, :, columns] = both.astype(jnp.bfloat16)
        for d in (2, 1, 3):
            return_column(n, d).start()

    for n in range(N_CHUNKS):
        columns = slice(n * N_CHUNK, (n + 1) * N_CHUNK)
        for e in range(2):
            produced = dot(r.hidden[e], r.dn[e, :, :, columns].reshape(FF, N_CHUNK))
            gates = r.slot_gates[e].reshape(4 * PART, 1)
            r.produced[e, :, :, :] = (produced * gates).astype(jnp.bfloat16).reshape(4, PART, N_CHUNK)
        for side in (1, 0):
            for d in range(4):
                rows = slice(side * SLOTS, (side + 1) * SLOTS)
                stacked = jnp.concatenate([r.produced[0, d, rows, :], r.produced[1, d, rows, :]], axis=0)
                back = lax.dot_general(
                    r.slots[d, side], stacked, (((0,), (0,)), ((), ())), preferred_element_type=jnp.float32
                )
                r.outgoing[side, d, :, columns] = back.astype(jnp.bfloat16)
            if side:
                return_core(n).start()
        if n:
            merge(n - 1)
    merge(N_CHUNKS - 1)
    for n in range(N_CHUNKS):
        columns = slice(n * N_CHUNK, (n + 1) * N_CHUNK)
        for d in (1, 2, 3):
            return_column(n, d).wait_recv()
        result = r.middle[:, columns].astype(jnp.float32) + r.merged[0, :, columns].astype(jnp.float32)
        for d in range(3):
            result = result + r.column_in[d, :, columns].astype(jnp.float32)
        r.out[:, columns] = result.astype(jnp.bfloat16)

    for i in range(len(moves)):
        weight_copy(i).wait_send()
    routing.wait_send()
    for d in (1, 2, 3):
        pair_copy(d).wait_send()
        partial_copy(d).wait_send()
        state_copy(d).wait_send()
    for d in range(4):
        across_copy(d).wait_send()
    for n in range(N_CHUNKS):
        return_core(n).wait_send()
        for d in (1, 2, 3):
            return_column(n, d).wait_send()


INPUTS = ("tokens", "segments", "gains", "query_weight", "pair_weight", "output_weight", "gu_own", "dn_own", "routing")


def layer(*operands):
    moves = gather_moves(PIECES)
    program = gather_program(moves, DEPTH)
    bf, wide = jnp.bfloat16, jnp.float32
    buffers = dict(
        normed=pltpu.VMEM((ROWS, MODEL_WIDTH), bf),
        pairs=pltpu.VMEM((WINDOW + ROWS, 256), bf),
        queries=pltpu.VMEM((ROWS, 384), bf),
        attended=pltpu.VMEM((ROWS, 384), bf),
        projected=pltpu.VMEM((4, PART, MODEL_WIDTH), bf),
        projected_in=pltpu.VMEM((3, PART, MODEL_WIDTH), bf),
        routing_other=pltpu.VMEM((4, 8, PART), wide),
        slots=pltpu.VMEM((4, 2, 2 * SLOTS, PART), bf),
        slot_gates=pltpu.VMEM((2, 4, PART, 1), wide),
        middle=pltpu.VMEM((PART, MODEL_WIDTH), bf),
        states=pltpu.VMEM((2, 4, PART, MODEL_WIDTH), bf),
        routed=pltpu.VMEM((2, 4, PART, MODEL_WIDTH), bf),
        hidden=pltpu.VMEM((2, 4 * PART, FF), bf),
        produced=pltpu.VMEM((2, 4, PART, N_CHUNK), bf),
        outgoing=pltpu.VMEM((2, 4, PART, MODEL_WIDTH), bf),
        core_in=pltpu.VMEM((4, PART, MODEL_WIDTH), bf),
        merged=pltpu.VMEM((4, PART, MODEL_WIDTH), bf),
        column_in=pltpu.VMEM((3, PART, MODEL_WIDTH), bf),
        gu=pltpu.VMEM((2, 16, 96, MODEL_WIDTH), bf),
        dn=pltpu.VMEM((2, 16, 48, MODEL_WIDTH), bf),
        own_sems=pltpu.SemaphoreType.DMA((2,)),
    )
    counts = dict(
        weight=len(moves), routing=1, pair=3, projected=3, state=3, across=4, core=N_CHUNKS, column=3 * N_CHUNKS
    )
    for name, count in counts.items():
        buffers[name + "_send"] = pltpu.SemaphoreType.DMA((count,))
        buffers[name + "_recv"] = pltpu.SemaphoreType.DMA((count,))
    names = INPUTS + ("out",) + tuple(buffers)

    def kernel(*refs):
        found = dict(zip(names, refs))
        for name in counts:
            found[name + "_sems"] = (found[name + "_send"], found[name + "_recv"])
        layer_kernel(moves, program, types.SimpleNamespace(**found))

    return pl.pallas_call(
        kernel,
        out_shape=jax.ShapeDtypeStruct((PART, MODEL_WIDTH), bf),
        in_specs=[pl.BlockSpec(memory_space=pltpu.VMEM)] * len(INPUTS),
        out_specs=pl.BlockSpec(memory_space=pltpu.VMEM),
        scratch_shapes=list(buffers.values()),
        compiler_params=pltpu.CompilerParams(
            collective_id=0, has_side_effects=True, vmem_limit_bytes=66_000_000
        ),
    )(*operands)


def body(
    tokens,
    segments,
    norm_gains,
    query_weight,
    key_value_matrix,
    output_weight,
    trainer_gateup,
    trainer_down,
    routes,
    route_weights,
):
    routing = jnp.concatenate(
        [routes.astype(jnp.float32).reshape(4, PART, TOPK), route_weights.reshape(4, PART, TOPK)], axis=2
    ).transpose(0, 2, 1)
    out = layer(
        tokens,
        segments.reshape(-1, 128),
        norm_gains,
        query_weight,
        key_value_matrix,
        output_weight,
        trainer_gateup[0].astype(jnp.bfloat16),
        trainer_down[0].astype(jnp.bfloat16),
        routing,
    )
    return out.reshape(1, 1, PART, MODEL_WIDTH)


def solution(mesh):
    in_specs = (
        P(("dp", "expert"), None),
        P(),
        P(),
        P(None, "mp"),
        P(),
        P("mp", None),
        P(("mp", "expert"), "dp", None),
        P(("mp", "expert"), "dp", None),
        P(("dp", "expert"), None),
        P(("dp", "expert"), None),
    )
    out_specs = P(("dp", "expert"), "mp", None, None)
    return jax.shard_map(body, mesh=mesh, in_specs=in_specs, out_specs=out_specs, check_vma=False)
```

time: 335 us -> 151 us (0.45)
  waiting for transfers between devices: 88.8 us -> 0 us
  starting transfers between devices: 31.9 us -> 0 us
  local copies, waits for them, and re-layouts: 33 us -> 2.57 us
  matrix products: 18.9 us -> 0 us
  between operations: 13.7 us -> 0.01 us
  other arithmetic: 14 us -> 4.76 us
  Pallas kernels: 134 us -> 141 us
    all_to_all x2 -> x0, waiting for transfers between devices: 58.6 us -> none  [the longest x1 58.6 us: body(): lax.all_to_all(produced, ('mp', 'expert'), split_axis=0, concat_axis=0, t...]
    reduce_scatter x1 -> x0, waiting for transfers between devices: 28.7 us -> none  [body(): lax.psum_scatter(jnp.dot(attended, output_weight, preferred_element_type=...]
    dot_general x7 -> x0, matrix products: 18.9 us -> none  [the longest x1 6.54 us: body(): jnp.dot(received.reshape(senders * slots_here, MODEL_WIDTH), gateup_full[...]
    ppermute x3 -> x0, starting transfers between devices: 17 us -> none  [shifted(): lax.ppermute(value, axis, [(source, source + steps) for source in range(i...]
    all_to_all x2 -> x0, starting transfers between devices: 15 us -> none  [the longest x1 7.67 us: body(): lax.all_to_all(produced, ('mp', 'expert'), split_axis=0, concat_axis=0, t...]
    gather x2 -> x0, local copies, waits for them, and re-layouts: 14 us -> none  [the longest x1 8.38 us: body(): key_segment = jnp.where(key_pos >= 0, segments[jnp.maximum(key_pos, 0)], -1)]
    dynamic_slice x6 -> x0, local copies, waits for them, and re-layouts: 9.27 us -> none  [the longest x2 8.21 us: body(): lax.dynamic_index_in_dim(both, half, 0, keepdims=True)]
    pallas_call x1, Pallas kernels: 134 us -> 141 us  [layer(): pl.pallas_call(kernel, out_shape=jax.ShapeDtypeStruct((PART, MODEL_WIDTH)...]
  transfers between devices with their start and end apart: 6 -> 0, of which waited for: 3 -> 0; matrix products, arithmetic and copies ran while one was open for 7% -> 0% of each run, Pallas kernels for 40% -> 0%
where the time goes in v2:
time: 151 us; the launch traced here: 149 us
  Pallas kernels  141 us (93%)
  other arithmetic  4.76 us (3%)
  local copies, waits for them, and re-layouts  2.57 us (2%)
    pallas_call x1, Pallas kernels, layer(): pl.pallas_call(kernel, out_shape=jax.ShapeDtypeStruct((PART, MODEL_WIDTH)...  141 us

profile of v2, /device:TPU:32, one launch (start us, length us, event | category | flops | bytes accessed | tf_op | source)
XLA Modules:
  0.0 148.8 jit_solution(12544291087412170287)
XLA Ops:
  0.0 0.7 convert_element_type.17
  0.7 0.1 reshape.15
  0.8 0.8 reshape.16
  1.6 0.6 maximum_bitcast_fusion.refs_8_
  2.2 1.6 %convert_bitcast_fusion.1.refs_7_ = bf16[48,1536]{1,0:T(8,128)(2,1)} fusion(f32[1,48,1536]{2,1,0:T(8,128)} %param.17), kind=kLoop, calls=%fused_computation.1 | loop fusion | flops 73728 | bytes 442368 | tf_op jit(solution)/shard_map/convert_element_type | solution.py:493
  3.8 1.8 %convert_bitcast_fusion.refs_6_ = bf16[96,1536]{1,0:T(8,128)(2,1)} fusion(f32[1,96,1536]{2,1,0:T(8,128)} %param.16), kind=kLoop, calls=%fused_computation | loop fusion | flops 147456 | bytes 884736 | tf_op jit(solution)/shard_map/convert_element_type | solution.py:492
  5.6 141.5 %shard_map.100 = bf16[96,1536]{1,0:T(8,128)(2,1)} custom-call(bf16[384,1536]{1,0:T(8,128)(2,1)} %refs_0_.1, s32[192,128]{1,0:T(8,128)} %bitcast.13, f32[2,1536]{1,0:T(2,128)} %refs_2_.1, bf16[1536,384]{1,0:T(8,128)(2,1)} %refs_3_.1, bf16[2,1536,256]{2,1,0:T(8,128)(2,1)} %refs_4_.1, bf16[384,1536]{1,0:T(8,128)(2,1)} %refs_5_.1, ...), custom_call_target="tpu_custom_call" | custom-call | tf_op jit(solution)/shard_map/pallas_call | solution.py:458
  147.1 1.7 %copy.14 = bf16[1,1,96,1536]{3,2,1,0:T(8,128)(2,1)} copy(bf16[1,1,96,1536]{3,2,1,0:T(8,128)(2,1)} %bitcast.12) | data formatting | bytes 589824
  (2 shorter events, 0.0 us)

commit v3 on v2

v3 whole, which is shorter than its diff:
```python
import functools
import heapq
import math
import types

import jax
import jax.numpy as jnp
from jax import lax
from jax.experimental import pallas as pl
from jax.experimental.pallas import tpu as pltpu
from jax.sharding import PartitionSpec as P

MODEL_WIDTH = 1536
FF = 768
TOPK = 4


LINKS = ("y+", "y-", "z+", "z-")
AXES = ("dp", "mp", "expert")
MESH = pl.DeviceIdType.MESH


def column_ring(moves, rank, tag, piece, halves, dy, have):
    got = {0: have}
    up, down = have, have
    for s in range(1, 4):
        moves.append(("z+", (dy, 1 - s), piece, up, (rank, tag, s)))
        up = got[-s] = [len(moves) - 1]
        moves.append(("z-", (dy, s - 1), piece, down, (rank, tag, s)))
        down = got[s] = [len(moves) - 1]
    moves.append(("z+", (dy, -3), halves[0], up, (rank, tag, 4)))
    moves.append(("z-", (dy, 3), halves[1], down, (rank, tag, 4)))
    got[4] = [len(moves) - 2, len(moves) - 1]
    return got


def row_ring(moves, rank, tag, piece, halves, dz, have, late):
    start = len(moves)
    moves.append(("y+", (0, dz), piece, have, (rank, tag, 1 + late)))
    moves.append(("y-", (0, dz), piece, have, (rank, tag, 1 + late)))
    moves.append(("y+", (-1, dz), halves[0], [start], (rank, tag, 2 + late)))
    moves.append(("y-", (1, dz), halves[1], [start + 1], (rank, tag, 2 + late)))
    return {0: have, -1: [start], 1: [start + 1], 2: [start + 2, start + 3]}


def gather_moves(pieces):
    moves = []
    for rank, order, piece, halves in pieces:
        if order == "zy":
            got = column_ring(moves, rank, 0, piece, halves, 0, [])
            for late, dz in enumerate((0, -1, 1, -2, 2, -3, 3, 4)):
                row_ring(moves, rank, 1, piece, halves, dz, got[dz], late)
        else:
            got = row_ring(moves, rank, 0, piece, halves, 0, [], 0)
            for late, dy in enumerate((0, -1, 1, 2)):
                column_ring(moves, rank, 1 + late, piece, halves, dy, got[dy])
    return moves


def gather_program(moves, rate=40e3, latency=1.7):
    issued, got = set(), set()
    free = dict.fromkeys(LINKS, 0.0)
    arrivals, now, program = [], 0.0, []
    while True:
        for link in LINKS:
            while True:
                ready = [
                    (moves[i][4], i)
                    for i in range(len(moves))
                    if moves[i][0] == link and i not in issued and got.issuperset(moves[i][3])
                ]
                if not ready:
                    break
                (rank, _, _), i = min(ready)
                if free[link] - now > (AHEAD_FIRST if rank == 0 else AHEAD):
                    break
                _, r0, r1, c0, c1 = moves[i][2]
                issued.add(i)
                program.append(("send", i, now))
                free[link] = max(now, free[link]) + (r1 - r0) * (c1 - c0) * 2 / rate
                heapq.heappush(arrivals, (free[link] + latency, i))
        if not arrivals:
            return program
        now, i = heapq.heappop(arrivals)
        got.add(i)
        program.append(("recv", i, now))


PIECES = (
    (0, "zy", ("gu", 0, 96, 0, 896), (("gu", 0, 48, 0, 896), ("gu", 48, 96, 0, 896))),
    (0, "yz", ("gu", 0, 96, 896, 1536), (("gu", 0, 48, 896, 1536), ("gu", 48, 96, 896, 1536))),
    (1, "zy", ("dn", 0, 48, 0, 256), (("dn", 0, 48, 0, 128), ("dn", 0, 48, 128, 256))),
    (1, "yz", ("dn", 0, 48, 256, 512), (("dn", 0, 48, 256, 384), ("dn", 0, 48, 384, 512))),
    (2, "zy", ("dn", 0, 48, 512, 1024), (("dn", 0, 48, 512, 768), ("dn", 0, 48, 768, 1024))),
    (3, "zy", ("dn", 0, 48, 1024, 1280), (("dn", 0, 48, 1024, 1152), ("dn", 0, 48, 1152, 1280))),
    (3, "yz", ("dn", 0, 48, 1280, 1536), (("dn", 0, 48, 1280, 1408), ("dn", 0, 48, 1408, 1536))),
)
AHEAD_FIRST = 30.0
AHEAD = 12.0
PUMP = {
    "start": 0.1, "pairs": 5.2, "query": 7.8, "onward": 15.6, "window": 23.4,
    "a00": 24.7, "a01": 26, "a02": 27.3, "a10": 28.6, "a11": 29.9, "a12": 31.2, "a20": 32.5, "a21": 33.8, "a22": 35.1,
    "project": 37.7, "slots": 41.6, "partial": 52, "middle": 55.9,
    "g0": 58.5, "g1": 63.7, "g2": 68.9, "g3": 72.8,
}

ROWS = 384
PART = 96
SLOTS = 48
WINDOW = 1152
F_CHUNK = 256
N_CHUNK = 512
N_CHUNKS = MODEL_WIDTH // N_CHUNK


def dot(a, b):
    return jnp.dot(a, b, preferred_element_type=jnp.float32)


def layer_kernel(moves, program, refs):
    r = refs
    dp, mp, expert = (lax.axis_index(a) for a in AXES)
    y, z_lo, z_hi, core = dp // 4, dp % 4, expert // 2, expert % 2
    z = z_hi * 4 + z_lo
    group = dp * 4 + expert

    def place(dy, dz):
        other_y, other_z = (y + dy + 8) % 4, (z + dz + 8) % 8
        return other_z // 4, other_y * 4 + other_z % 4

    def grid_device(dy, dz):
        half, index = place(dy, dz)
        return (index, mp, half * 2 + core)

    def column_device(d):
        return (dp, (mp + d + 4) % 4, expert)

    def piece_device(d):
        other = (group + d + 64) % 64
        return (other // 4, mp, other % 4)

    partner = (dp, mp, z_hi * 2 + 1 - core)
    target = {"y+": (1, 0), "y-": (-1, 0), "z+": (0, 1), "z-": (0, -1)}

    barrier = pltpu.get_barrier_semaphore()
    greeted = [grid_device(*target[link]) for link in LINKS]
    beside = (dp, mp + 1 - 2 * (mp % 2), expert)
    across = (dp, mp + 1 - 2 * (mp % 2), z_hi * 2 + 1 - core)
    greeted += [column_device(d) for d in (1, 2, 3)] + [partner, across]
    greeted += [piece_device(-2), piece_device(2 * core - 3)]
    for other in greeted:
        pl.semaphore_signal(barrier, inc=1, device_id=other, device_id_type=MESH)
    sent = []

    class Transfer:
        def __init__(self, start, landing, sems, i, device):
            self.copy = pltpu.make_async_remote_copy(
                src_ref=start,
                dst_ref=landing,
                send_sem=sems[0].at[i],
                recv_sem=sems[1].at[i],
                device_id=device,
                device_id_type=MESH,
            )

        def start(self):
            self.copy.start()
            sent.append(self)

        def wait_recv(self):
            self.copy.wait_recv()

    remote = Transfer

    whole = {"gu": r.gu, "dn": r.dn}

    def weight_copy(i):
        link, (dy, dz), (name, r0, r1, c0, c1), _, _ = moves[i]
        half, index = place(dy, dz)
        slab = whole[name].at[half, index, pl.ds(r0, r1 - r0), pl.ds(c0, c1 - c0)]
        return remote(slab, slab, r.weight_sems, i, grid_device(*target[link]))

    position = [0]

    def advance(stop):
        while position[0] < len(program) and not stop(program[position[0]]):
            kind, i, _ = program[position[0]]
            if kind == "send":
                weight_copy(i).start()
            else:
                weight_copy(i).wait_recv()
            position[0] += 1

    def pump(name):
        advance(lambda step: step[2] > PUMP[name])

    def pump_for(span):
        if position[0] < len(program):
            end = program[position[0]][2] + span
            advance(lambda step: step[2] > end)

    def have(name, columns):
        needed = {
            i for i, move in enumerate(moves)
            if move[2][0] == name and move[2][3] < columns[1] and columns[0] < move[2][4]
        }
        needed -= {i for kind, i, _ in program[: position[0]] if kind == "recv"}

        def stop(step):
            if not needed:
                return True
            if step[0] == "recv":
                needed.discard(step[1])
            return False

        advance(stop)

    half, index = place(0, 0)
    arriving = {}
    for k, name in enumerate(LOADED):
        start = getattr(r, name)
        if name == "pair_weight":
            start = start.at[mp // 2]
        arriving[name] = pltpu.make_async_copy(start, getattr(r, name + "_here"), r.load_sems.at[k])
        arriving[name].start()
    arriving["trainer_gateup"].wait()
    r.gu[half, index] = r.trainer_gateup_here[...].astype(jnp.bfloat16)
    arriving["trainer_down"].wait()
    r.dn[half, index] = r.trainer_down_here[...].astype(jnp.bfloat16)
    barrier = pltpu.get_barrier_semaphore()
    pl.semaphore_wait(barrier, len(greeted))
    routing = [
        remote(here, there, r.routing_sems, k, partner)
        for k, (here, there) in enumerate(((r.routes, r.routes_other), (r.gates, r.gates_other)))
    ]
    for copy in routing:
        copy.start()
    pump("start")

    arriving["tokens"].wait()
    gain = r.gains[0:1, :]

    @pl.loop(0, ROWS // 32)
    def _(i):
        rows = pl.ds(pl.multiple_of(i * 32, 32), 32)
        wide = r.tokens_here[rows, :].astype(jnp.float32)
        scale = lax.rsqrt(jnp.mean(wide * wide, axis=-1, keepdims=True) + 1e-6)
        r.normed[rows, :] = (wide * scale * gain).astype(jnp.bfloat16)

    arriving["pair_weight"].wait()
    pair = dot(r.normed[...], r.pair_weight_here[...]).astype(jnp.bfloat16)
    for part in range(2):
        r.pairs[part, WINDOW:, :] = pair[:, part * 128 : (part + 1) * 128]

    half_here = mp % 2

    def piece_rows(k):
        return pl.ds(pl.multiple_of(k * ROWS, ROWS), ROWS)

    onward = remote(
        r.pairs.at[half_here, piece_rows(3)], r.pairs.at[half_here, piece_rows(1)], r.pair_sems, 0, piece_device(2)
    )
    direct = remote(
        r.pairs.at[:, piece_rows(3)],
        r.pairs.at[:, piece_rows(2 - 2 * core)],
        r.pair_sems,
        1,
        piece_device(1 + 2 * core),
    )
    landed = r.pairs.at[half_here, piece_rows(1)]
    crossing = r.pairs.at[half_here, piece_rows(2 * core)]
    shares = [
        remote(landed, landed, r.pair_sems, 2, beside),
        remote(landed, crossing, r.pair_sems, 3, partner),
        remote(landed, crossing, r.pair_sems, 4, across),
    ]
    onward.start()
    direct.start()
    pump("pairs")
    arriving["query_weight"].wait()
    r.queries[...] = dot(r.normed[...], r.query_weight_here[...]).astype(jnp.bfloat16)
    pump("query")

    lanes = []
    for k in range(12):
        row = (group * 3 - 9 + k + 192) % 192
        lanes.append(r.segments[pl.ds(row, 1), :])
    key_segment = jnp.concatenate(lanes, axis=1)
    diagonal = lax.broadcasted_iota(jnp.int32, (128, 128), 0) == lax.broadcasted_iota(
        jnp.int32, (128, 128), 1
    )
    first_key = (group - 3) * ROWS

    pump("onward")
    onward.wait_recv()
    for copy in shares:
        copy.start()
    pump("window")
    for copy in shares + [direct]:
        copy.wait_recv()
    for c in range(3):
        low = (c + 1) * 128
        own_lanes = jnp.broadcast_to(lanes[9 + c].astype(jnp.float32), (128, 128))
        query_segment = jnp.sum(jnp.where(diagonal, own_lanes, 0.0), axis=1, keepdims=True)
        key_offset = low + lax.broadcasted_iota(jnp.int32, (128, WINDOW), 1)
        query_offset = WINDOW + c * 128 + lax.broadcasted_iota(jnp.int32, (128, WINDOW), 0)
        allowed = (
            (key_segment[:, low : low + WINDOW].astype(jnp.float32) == query_segment)
            & (key_offset <= query_offset)
            & (key_offset + first_key >= 0)
        )
        keys = r.pairs[0, low : low + WINDOW, :]
        values = r.pairs[1, low : low + WINDOW, :]
        for h in range(3):
            query = r.queries[c * 128 : (c + 1) * 128, h * 128 : (h + 1) * 128]
            scores = lax.dot_general(
                query, keys, (((1,), (1,)), ((), ())), preferred_element_type=jnp.float32
            )
            scores = jnp.where(allowed, scores * (1.0 / math.sqrt(128)), -1e30)
            weights = jnp.exp(scores - jnp.max(scores, axis=1, keepdims=True))
            total = jnp.sum(weights, axis=1, keepdims=True)
            mixed = dot(weights.astype(jnp.bfloat16), values) / total
            r.attended[c * 128 : (c + 1) * 128, h * 128 : (h + 1) * 128] = mixed.astype(jnp.bfloat16)
            pump(f"a{c}{h}")

    def partial_copy(d):
        return remote(
            r.projected.at[(mp + d) % 4], r.projected_in.at[d - 1], r.projected_sems, d - 1, column_device(d)
        )

    arriving["output_weight"].wait()
    r.projected[...] = (
        dot(r.attended[...], r.output_weight_here[...]).astype(jnp.bfloat16).reshape(4, PART, MODEL_WIDTH)
    )
    for d in (2, 1, 3):
        partial_copy(d).start()
    pump("project")

    for copy in routing:
        copy.wait_recv()
    before = lax.broadcasted_iota(jnp.int32, (ROWS, ROWS), 0)
    token = lax.broadcasted_iota(jnp.int32, (ROWS, ROWS), 1)
    earlier = ((before < token) & (before // PART == token // PART)).astype(jnp.bfloat16)
    slot = lax.broadcasted_iota(jnp.int32, (SLOTS, ROWS), 0).astype(jnp.float32)
    for side, (routes, gates) in enumerate(((r.routes, r.gates), (r.routes_other, r.gates_other))):
        for e in range(2):
            named = routes[...] == mp * 4 + e * 2 + core
            hit = jnp.sum(jnp.where(named, 1.0, 0.0), axis=0, keepdims=True)
            gate = jnp.sum(jnp.where(named, gates[...], 0.0), axis=0, keepdims=True)
            rank = dot(jnp.broadcast_to(hit, (8, ROWS)).astype(jnp.bfloat16), earlier)[0:1, :]
            chosen = jnp.where((slot == rank) & (hit > 0.5), 1.0, 0.0)
            weighed = chosen * gate
            for m in range(4):
                lanes = slice(m * PART, (m + 1) * PART)
                r.slots[m, side, e * SLOTS : (e + 1) * SLOTS, :] = chosen[:, lanes].astype(jnp.bfloat16)
                r.slot_gates[e, m, side * SLOTS : (side + 1) * SLOTS, :] = jnp.sum(
                    weighed[:, lanes], axis=1, keepdims=True
                )
    pump("slots")
    pump("partial")

    for d in (1, 2, 3):
        partial_copy(d).wait_recv()
    summed = r.tokens_here[pl.ds(pl.multiple_of(mp * PART, PART), PART), :].astype(jnp.float32)
    attention = r.projected[mp].astype(jnp.float32)
    for d in range(3):
        attention = attention + r.projected_in[d].astype(jnp.float32)
    middle = (summed + attention).astype(jnp.bfloat16)
    r.middle[...] = middle
    wide = middle.astype(jnp.float32)
    scale = lax.rsqrt(jnp.mean(wide * wide, axis=-1, keepdims=True) + 1e-6)
    r.states[0, 0] = (wide * scale * r.gains[1:2, :]).astype(jnp.bfloat16)

    def state_copy(d):
        return remote(r.states.at[0, 0], r.states.at[0, d], r.state_sems, d - 1, column_device(d))

    def across_copy(d):
        return remote(r.states.at[0, d], r.states.at[1, d], r.across_sems, d, partner)

    for d in (2, 1, 3):
        state_copy(d).start()
    across_copy(0).start()
    pump("middle")
    for step, d in enumerate((0, 1, 3, 2)):
        pump(f"g{step}")
        if d:
            state_copy(d).wait_recv()
            across_copy(d).start()
        for side in range(2):
            if side:
                across_copy(d).wait_recv()
            picked = dot(r.slots[(mp - d + 4) % 4, side], r.states[side, d]).astype(jnp.bfloat16)
            for e in range(2):
                r.routed[e, d, side * SLOTS : (side + 1) * SLOTS, :] = picked[e * SLOTS : (e + 1) * SLOTS]

    have("gu", (0, MODEL_WIDTH))
    for e in range(2):
        inputs = r.routed[e].reshape(4 * PART, MODEL_WIDTH)
        for f in range(3):
            left = f * F_CHUNK
            gate = dot(inputs, r.gu[e, :, :, left : left + F_CHUNK].reshape(MODEL_WIDTH, F_CHUNK))
            rise = dot(inputs, r.gu[e, :, :, FF + left : FF + left + F_CHUNK].reshape(MODEL_WIDTH, F_CHUNK))
            r.hidden[e, :, left : left + F_CHUNK] = (jnp.maximum(gate, 0.0) * rise).astype(jnp.bfloat16)
            pump_for(0.7)

    def return_core(n):
        columns = pl.ds(n * N_CHUNK, N_CHUNK)
        return remote(
            r.outgoing.at[1, :, :, columns], r.core_in.at[:, :, columns], r.core_sems, n, partner
        )

    def return_column(n, d):
        columns = pl.ds(n * N_CHUNK, N_CHUNK)
        return remote(
            r.merged.at[d, :, columns],
            r.column_in.at[d - 1, :, columns],
            r.column_sems,
            n * 3 + d - 1,
            column_device(-d),
        )

    def merge(n):
        columns = slice(n * N_CHUNK, (n + 1) * N_CHUNK)
        return_core(n).wait_recv()
        for d in (2, 1, 3, 0):
            both = r.outgoing[0, d, :, columns].astype(jnp.float32) + r.core_in[d, :, columns].astype(
                jnp.float32
            )
            r.merged[d, :, columns] = both.astype(jnp.bfloat16)
        for d in (2, 1, 3):
            return_column(n, d).start()

    for n in range(N_CHUNKS):
        columns = slice(n * N_CHUNK, (n + 1) * N_CHUNK)
        have("dn", (n * N_CHUNK, (n + 1) * N_CHUNK))
        for e in range(2):
            produced = dot(r.hidden[e], r.dn[e, :, :, columns].reshape(FF, N_CHUNK))
            for d in range(4):
                rows = produced[d * PART : (d + 1) * PART] * r.slot_gates[e, (mp - d + 4) % 4]
                r.produced[e, d] = rows.astype(jnp.bfloat16)
            pump_for(0.8)
        for side in (1, 0):
            for d in range(4):
                rows = slice(side * SLOTS, (side + 1) * SLOTS)
                stacked = jnp.concatenate([r.produced[0, d, rows, :], r.produced[1, d, rows, :]], axis=0)
                back = lax.dot_general(
                    r.slots[(mp - d + 4) % 4, side], stacked, (((0,), (0,)), ((), ())), preferred_element_type=jnp.float32
                )
                r.outgoing[side, d, :, columns] = back.astype(jnp.bfloat16)
            if side:
                return_core(n).start()
            pump_for(0.8)
        if n:
            merge(n - 1)
    merge(N_CHUNKS - 1)
    for n in range(N_CHUNKS):
        columns = slice(n * N_CHUNK, (n + 1) * N_CHUNK)
        for d in (1, 2, 3):
            return_column(n, d).wait_recv()
        result = r.middle[:, columns].astype(jnp.float32) + r.merged[0, :, columns].astype(jnp.float32)
        for d in range(3):
            result = result + r.column_in[d, :, columns].astype(jnp.float32)
        r.out[:, columns] = result.astype(jnp.bfloat16)

    for copy in sent:
        copy.copy.wait_send()


LOADED = ("trainer_gateup", "trainer_down", "tokens", "pair_weight", "query_weight", "output_weight")
INPUTS = LOADED + ("segments", "gains", "routes", "gates")


def layer(*operands):
    moves = gather_moves(PIECES)
    program = gather_program(moves)
    bf, wide = jnp.bfloat16, jnp.float32
    buffers = dict(
        normed=pltpu.VMEM((ROWS, MODEL_WIDTH), bf),
        pairs=pltpu.VMEM((2, WINDOW + ROWS, 128), bf),
        queries=pltpu.VMEM((ROWS, 384), bf),
        attended=pltpu.VMEM((ROWS, 384), bf),
        projected=pltpu.VMEM((4, PART, MODEL_WIDTH), bf),
        projected_in=pltpu.VMEM((3, PART, MODEL_WIDTH), bf),
        routes_other=pltpu.VMEM((TOPK, ROWS), jnp.int32),
        gates_other=pltpu.VMEM((TOPK, ROWS), wide),
        slots=pltpu.VMEM((4, 2, 2 * SLOTS, PART), bf),
        slot_gates=pltpu.VMEM((2, 4, PART, 1), wide),
        middle=pltpu.VMEM((PART, MODEL_WIDTH), bf),
        states=pltpu.VMEM((2, 4, PART, MODEL_WIDTH), bf),
        routed=pltpu.VMEM((2, 4, PART, MODEL_WIDTH), bf),
        hidden=pltpu.VMEM((2, 4 * PART, FF), bf),
        produced=pltpu.VMEM((2, 4, PART, N_CHUNK), bf),
        outgoing=pltpu.VMEM((2, 4, PART, MODEL_WIDTH), bf),
        core_in=pltpu.VMEM((4, PART, MODEL_WIDTH), bf),
        merged=pltpu.VMEM((4, PART, MODEL_WIDTH), bf),
        column_in=pltpu.VMEM((3, PART, MODEL_WIDTH), bf),
        gu=pltpu.VMEM((2, 16, 96, MODEL_WIDTH), bf),
        dn=pltpu.VMEM((2, 16, 48, MODEL_WIDTH), bf),
        load_sems=pltpu.SemaphoreType.DMA((len(LOADED),)),
    )
    for name, operand in zip(LOADED, operands):
        shape = operand.shape[1:] if name == "pair_weight" else operand.shape
        buffers[name + "_here"] = pltpu.VMEM(shape, operand.dtype)
    counts = dict(
        weight=len(moves), routing=2, pair=5, projected=3, state=3, across=4, core=N_CHUNKS, column=3 * N_CHUNKS
    )
    for name, count in counts.items():
        buffers[name + "_send"] = pltpu.SemaphoreType.DMA((count,))
        buffers[name + "_recv"] = pltpu.SemaphoreType.DMA((count,))
    names = INPUTS + ("out",) + tuple(buffers)

    def kernel(*refs):
        found = dict(zip(names, refs))
        for name in counts:
            found[name + "_sems"] = (found[name + "_send"], found[name + "_recv"])
        layer_kernel(moves, program, types.SimpleNamespace(**found))

    return pl.pallas_call(
        kernel,
        out_shape=jax.ShapeDtypeStruct((PART, MODEL_WIDTH), bf),
        in_specs=[
            pl.BlockSpec(memory_space=pl.ANY if name in LOADED else pltpu.VMEM) for name in INPUTS
        ],
        out_specs=pl.BlockSpec(memory_space=pltpu.VMEM),
        scratch_shapes=list(buffers.values()),
        compiler_params=pltpu.CompilerParams(
            collective_id=0, has_side_effects=True, vmem_limit_bytes=66_000_000
        ),
    )(*operands)


def body(
    tokens,
    segments,
    norm_gains,
    query_weight,
    key_value_matrix,
    output_weight,
    trainer_gateup,
    trainer_down,
    routes,
    route_weights,
):
    out = layer(
        trainer_gateup[0],
        trainer_down[0],
        tokens,
        key_value_matrix,
        query_weight,
        output_weight,
        segments.reshape(-1, 128),
        norm_gains,
        routes.T,
        route_weights.T,
    )
    return out.reshape(1, 1, PART, MODEL_WIDTH)


def solution(mesh):
    in_specs = (
        P(("dp", "expert"), None),
        P(),
        P(),
        P(None, "mp"),
        P(),
        P("mp", None),
        P(("mp", "expert"), "dp", None),
        P(("mp", "expert"), "dp", None),
        P(("dp", "expert"), None),
        P(("dp", "expert"), None),
    )
    out_specs = P(("dp", "expert"), "mp", None, None)
    return jax.shard_map(body, mesh=mesh, in_specs=in_specs, out_specs=out_specs, check_vma=False)
```

time: 151 us -> 121 us (0.80); the launches traced: 149 us -> 121 us
  Pallas kernels: 141 us -> 119 us
  other arithmetic: 4.76 us -> 0 us
    pallas_call x1, Pallas kernels: 141 us -> 119 us  [layer(): pl.pallas_call(kernel, out_shape=jax.ShapeDtypeStruct((PART, MODEL_WIDTH)...]
    convert_element_type x3 -> x0, other arithmetic: 4.15 us -> none  [the longest x1 1.81 us: body(): trainer_gateup[0].astype(jnp.bfloat16)]
where the time goes in v3:
time: 121 us
  Pallas kernels  119 us (98%)
  local copies, waits for them, and re-layouts  1.69 us (1%)
    pallas_call x1, Pallas kernels, layer(): pl.pallas_call(kernel, out_shape=jax.ShapeDtypeStruct((PART, MODEL_WIDTH)...  119 us

profile of v3, /device:TPU:32, one launch (start us, length us, event | category | flops | bytes accessed | tf_op | source)
XLA Modules:
  0.0 121.2 jit_solution(11970747318234511714)
XLA Ops:
  0.0 119.5 %shard_map.100 = bf16[96,1536]{1,0:T(8,128)(2,1)} custom-call(f32[96,1536]{1,0:T(8,128)} %bitcast.7, f32[48,1536]{1,0:T(8,128)} %bitcast.8, bf16[384,1536]{1,0:T(8,128)(2,1)} %refs_2_.1, bf16[2,1536,256]{2,1,0:T(8,128)(2,1)} %refs_3_.1, bf16[1536,384]{1,0:T(8,128)(2,1)} %refs_4_.1, bf16[384,1536]{1,0:T(8,128)(2,1)} %refs_5_.1, s32[192,128]{1,0:T(8,128)} %bitcast.9, ...), custom_call_target="tpu_custom_call" | custom-call | tf_op jit(solution)/shard_map/pallas_call | solution.py:518
  119.5 1.7 %copy.12 = bf16[1,1,96,1536]{3,2,1,0:T(8,128)(2,1)} copy(bf16[1,1,96,1536]{3,2,1,0:T(8,128)(2,1)} %bitcast.6) | data formatting | bytes 589824

commit v4 on v3

--- a/solution.py
+++ b/solution.py
@@ -87,21 +87,18 @@
 
 
 PIECES = (
-    (0, "zy", ("gu", 0, 96, 0, 896), (("gu", 0, 48, 0, 896), ("gu", 48, 96, 0, 896))),
-    (0, "yz", ("gu", 0, 96, 896, 1536), (("gu", 0, 48, 896, 1536), ("gu", 48, 96, 896, 1536))),
-    (1, "zy", ("dn", 0, 48, 0, 256), (("dn", 0, 48, 0, 128), ("dn", 0, 48, 128, 256))),
-    (1, "yz", ("dn", 0, 48, 256, 512), (("dn", 0, 48, 256, 384), ("dn", 0, 48, 384, 512))),
-    (2, "zy", ("dn", 0, 48, 512, 1024), (("dn", 0, 48, 512, 768), ("dn", 0, 48, 768, 1024))),
-    (3, "zy", ("dn", 0, 48, 1024, 1280), (("dn", 0, 48, 1024, 1152), ("dn", 0, 48, 1152, 1280))),
-    (3, "yz", ("dn", 0, 48, 1280, 1536), (("dn", 0, 48, 1280, 1408), ("dn", 0, 48, 1408, 1536))),
+    (0, "zy", ("gu", 0, 64, 0, 1536), (("gu", 0, 32, 0, 1536), ("gu", 32, 64, 0, 1536))),
+    (0, "yz", ("gu", 64, 96, 0, 1536), (("gu", 64, 80, 0, 1536), ("gu", 80, 96, 0, 1536))),
+    (1, "zy", ("dn", 0, 48, 0, 768), (("dn", 0, 48, 0, 384), ("dn", 0, 48, 384, 768))),
+    (1, "yz", ("dn", 0, 48, 768, 1536), (("dn", 0, 48, 768, 1152), ("dn", 0, 48, 1152, 1536))),
 )
 AHEAD_FIRST = 30.0
 AHEAD = 12.0
 PUMP = {
-    "start": 0.1, "pairs": 5.2, "query": 7.8, "onward": 15.6, "window": 23.4,
-    "a00": 24.7, "a01": 26, "a02": 27.3, "a10": 28.6, "a11": 29.9, "a12": 31.2, "a20": 32.5, "a21": 33.8, "a22": 35.1,
-    "project": 37.7, "slots": 41.6, "partial": 52, "middle": 55.9,
-    "g0": 58.5, "g1": 63.7, "g2": 68.9, "g3": 72.8,
+    "start": 0.1, "pairs": 4.4, "query": 6.6, "onward": 13.3, "window": 19.9,
+    "a00": 21.0, "a01": 22.1, "a02": 23.2, "a10": 24.3, "a11": 25.4, "a12": 26.5, "a20": 27.6, "a21": 28.7, "a22": 29.8,
+    "project": 32.0, "slots": 35.4, "partial": 44.2, "middle": 47.5,
+    "g0": 49.7, "g1": 60.5, "g2": 65.5, "g3": 69.2,
 }
 
 ROWS = 384
@@ -109,8 +106,7 @@
 SLOTS = 48
 WINDOW = 1152
 F_CHUNK = 256
-N_CHUNK = 512
-N_CHUNKS = MODEL_WIDTH // N_CHUNK
+BLOCKS = ((0, 512), (512, 896), (896, 1280), (1280, 1536))
 
 
 def dot(a, b):
@@ -343,12 +339,14 @@
     earlier = ((before < token) & (before // PART == token // PART)).astype(jnp.bfloat16)
     slot = lax.broadcasted_iota(jnp.int32, (SLOTS, ROWS), 0).astype(jnp.float32)
     for side, (routes, gates) in enumerate(((r.routes, r.gates), (r.routes_other, r.gates_other))):
+        picks = []
         for e in range(2):
             named = routes[...] == mp * 4 + e * 2 + core
             hit = jnp.sum(jnp.where(named, 1.0, 0.0), axis=0, keepdims=True)
             gate = jnp.sum(jnp.where(named, gates[...], 0.0), axis=0, keepdims=True)
             rank = dot(jnp.broadcast_to(hit, (8, ROWS)).astype(jnp.bfloat16), earlier)[0:1, :]
             chosen = jnp.where((slot == rank) & (hit > 0.5), 1.0, 0.0)
+            picks.append(chosen)
             weighed = chosen * gate
             for m in range(4):
                 lanes = slice(m * PART, (m + 1) * PART)
@@ -356,6 +354,9 @@
                 r.slot_gates[e, m, side * SLOTS : (side + 1) * SLOTS, :] = jnp.sum(
                     weighed[:, lanes], axis=1, keepdims=True
                 )
+        for m in range(4):
+            both = jnp.concatenate([chosen[:, m * PART : (m + 1) * PART] for chosen in picks], axis=0)
+            r.slots_back[m, side] = both.T.astype(jnp.bfloat16)
     pump("slots")
     pump("partial")
 
@@ -404,13 +405,13 @@
             pump_for(0.7)
 
     def return_core(n):
-        columns = pl.ds(n * N_CHUNK, N_CHUNK)
+        columns = pl.ds(BLOCKS[n][0], BLOCKS[n][1] - BLOCKS[n][0])
         return remote(
             r.outgoing.at[1, :, :, columns], r.core_in.at[:, :, columns], r.core_sems, n, partner
         )
 
     def return_column(n, d):
-        columns = pl.ds(n * N_CHUNK, N_CHUNK)
+        columns = pl.ds(BLOCKS[n][0], BLOCKS[n][1] - BLOCKS[n][0])
         return remote(
             r.merged.at[d, :, columns],
             r.column_in.at[d - 1, :, columns],
@@ -420,7 +421,7 @@
         )
 
     def merge(n):
-        columns = slice(n * N_CHUNK, (n + 1) * N_CHUNK)
+        columns = slice(*BLOCKS[n])
         return_core(n).wait_recv()
         for d in (2, 1, 3, 0):
             both = r.outgoing[0, d, :, columns].astype(jnp.float32) + r.core_in[d, :, columns].astype(
@@ -430,31 +431,31 @@
         for d in (2, 1, 3):
             return_column(n, d).start()
 
-    for n in range(N_CHUNKS):
-        columns = slice(n * N_CHUNK, (n + 1) * N_CHUNK)
-        have("dn", (n * N_CHUNK, (n + 1) * N_CHUNK))
+    for n in range(len(BLOCKS)):
+        columns = slice(*BLOCKS[n])
+        width = BLOCKS[n][1] - BLOCKS[n][0]
+        have("dn", BLOCKS[n])
         for e in range(2):
-            produced = dot(r.hidden[e], r.dn[e, :, :, columns].reshape(FF, N_CHUNK))
+            produced = dot(r.hidden[e], r.dn[e, :, :, columns].reshape(FF, width))
             for d in range(4):
                 rows = produced[d * PART : (d + 1) * PART] * r.slot_gates[e, (mp - d + 4) % 4]
-                r.produced[e, d] = rows.astype(jnp.bfloat16)
+                for side in range(2):
+                    r.produced[d, side, e * SLOTS : (e + 1) * SLOTS, :width] = rows[
+                        side * SLOTS : (side + 1) * SLOTS
+                    ].astype(jnp.bfloat16)
             pump_for(0.8)
         for side in (1, 0):
             for d in range(4):
-                rows = slice(side * SLOTS, (side + 1) * SLOTS)
-                stacked = jnp.concatenate([r.produced[0, d, rows, :], r.produced[1, d, rows, :]], axis=0)
-                back = lax.dot_general(
-                    r.slots[(mp - d + 4) % 4, side], stacked, (((0,), (0,)), ((), ())), preferred_element_type=jnp.float32
-                )
+                back = dot(r.slots_back[(mp - d + 4) % 4, side], r.produced[d, side, :, :width])
                 r.outgoing[side, d, :, columns] = back.astype(jnp.bfloat16)
             if side:
                 return_core(n).start()
             pump_for(0.8)
         if n:
             merge(n - 1)
-    merge(N_CHUNKS - 1)
-    for n in range(N_CHUNKS):
-        columns = slice(n * N_CHUNK, (n + 1) * N_CHUNK)
+    merge(len(BLOCKS) - 1)
+    for n in range(len(BLOCKS)):
+        columns = slice(*BLOCKS[n])
         for d in (1, 2, 3):
             return_column(n, d).wait_recv()
         result = r.middle[:, columns].astype(jnp.float32) + r.merged[0, :, columns].astype(jnp.float32)
@@ -484,12 +485,13 @@
         routes_other=pltpu.VMEM((TOPK, ROWS), jnp.int32),
         gates_other=pltpu.VMEM((TOPK, ROWS), wide),
         slots=pltpu.VMEM((4, 2, 2 * SLOTS, PART), bf),
+        slots_back=pltpu.VMEM((4, 2, PART, 2 * SLOTS), bf),
         slot_gates=pltpu.VMEM((2, 4, PART, 1), wide),
         middle=pltpu.VMEM((PART, MODEL_WIDTH), bf),
         states=pltpu.VMEM((2, 4, PART, MODEL_WIDTH), bf),
         routed=pltpu.VMEM((2, 4, PART, MODEL_WIDTH), bf),
         hidden=pltpu.VMEM((2, 4 * PART, FF), bf),
-        produced=pltpu.VMEM((2, 4, PART, N_CHUNK), bf),
+        produced=pltpu.VMEM((4, 2, 2 * SLOTS, max(b - a for a, b in BLOCKS)), bf),
         outgoing=pltpu.VMEM((2, 4, PART, MODEL_WIDTH), bf),
         core_in=pltpu.VMEM((4, PART, MODEL_WIDTH), bf),
         merged=pltpu.VMEM((4, PART, MODEL_WIDTH), bf),
@@ -502,7 +504,7 @@
         shape = operand.shape[1:] if name == "pair_weight" else operand.shape
         buffers[name + "_here"] = pltpu.VMEM(shape, operand.dtype)
     counts = dict(
-        weight=len(moves), routing=2, pair=5, projected=3, state=3, across=4, core=N_CHUNKS, column=3 * N_CHUNKS
+        weight=len(moves), routing=2, pair=5, projected=3, state=3, across=4, core=len(BLOCKS), column=3 * len(BLOCKS)
     )
     for name, count in counts.items():
         buffers[name + "_send"] = pltpu.SemaphoreType.DMA((count,))

time: 121 us -> 121 us (level)
  no operation moved by 1% of the time
where the time goes in v4:
time: 121 us; the launch traced here: 120 us
  Pallas kernels  118 us (98%)
  local copies, waits for them, and re-layouts  1.69 us (1%)
    pallas_call x1, Pallas kernels, layer(): pl.pallas_call(kernel, out_shape=jax.ShapeDtypeStruct((PART, MODEL_WIDTH)...  118 us

profile of v4, /device:TPU:32, one launch (start us, length us, event | category | flops | bytes accessed | tf_op | source)
XLA Modules:
  0.0 120.0 jit_solution(10048186404294941426)
XLA Ops:
  0.0 118.3 %shard_map.100 = bf16[96,1536]{1,0:T(8,128)(2,1)} custom-call(f32[96,1536]{1,0:T(8,128)} %bitcast.7, f32[48,1536]{1,0:T(8,128)} %bitcast.8, bf16[384,1536]{1,0:T(8,128)(2,1)} %refs_2_.1, bf16[2,1536,256]{2,1,0:T(8,128)(2,1)} %refs_3_.1, bf16[1536,384]{1,0:T(8,128)(2,1)} %refs_4_.1, bf16[384,1536]{1,0:T(8,128)(2,1)} %refs_5_.1, s32[192,128]{1,0:T(8,128)} %bitcast.9, ...), custom_call_target="tpu_custom_call" | custom-call | tf_op jit(solution)/shard_map/pallas_call | solution.py:520
  118.3 1.7 %copy.12 = bf16[1,1,96,1536]{3,2,1,0:T(8,128)(2,1)} copy(bf16[1,1,96,1536]{3,2,1,0:T(8,128)(2,1)} %bitcast.6) | data formatting | bytes 589824

commit v5 on v4

--- a/solution.py
+++ b/solution.py
@@ -106,7 +106,7 @@
 SLOTS = 48
 WINDOW = 1152
 F_CHUNK = 256
-BLOCKS = ((0, 512), (512, 896), (896, 1280), (1280, 1536))
+BLOCKS = ((0, 512), (512, 896), (896, 1152), (1152, 1408), (1408, 1536))
 
 
 def dot(a, b):

time: 121 us -> 120 us (level)
  no operation moved by 1% of the time
where the time goes in v5:
time: 120 us
  Pallas kernels  118 us (98%)
  local copies, waits for them, and re-layouts  1.69 us (1%)
    pallas_call x1, Pallas kernels, layer(): pl.pallas_call(kernel, out_shape=jax.ShapeDtypeStruct((PART, MODEL_WIDTH)...  118 us

profile of v5, /device:TPU:32, one launch (start us, length us, event | category | flops | bytes accessed | tf_op | source)
XLA Modules:
  0.0 120.1 jit_solution(8143638275208864232)
XLA Ops:
  0.0 118.4 %shard_map.100 = bf16[96,1536]{1,0:T(8,128)(2,1)} custom-call(f32[96,1536]{1,0:T(8,128)} %bitcast.7, f32[48,1536]{1,0:T(8,128)} %bitcast.8, bf16[384,1536]{1,0:T(8,128)(2,1)} %refs_2_.1, bf16[2,1536,256]{2,1,0:T(8,128)(2,1)} %refs_3_.1, bf16[1536,384]{1,0:T(8,128)(2,1)} %refs_4_.1, bf16[384,1536]{1,0:T(8,128)(2,1)} %refs_5_.1, s32[192,128]{1,0:T(8,128)} %bitcast.9, ...), custom_call_target="tpu_custom_call" | custom-call | tf_op jit(solution)/shard_map/pallas_call | solution.py:520
  118.4 1.7 %copy.12 = bf16[1,1,96,1536]{3,2,1,0:T(8,128)(2,1)} copy(bf16[1,1,96,1536]{3,2,1,0:T(8,128)(2,1)} %bitcast.6) | data formatting | bytes 589824
